TPU v7x, 512 devices: a whole 4x4x16 slice. The times are simulated.
512 devices in a mesh: seq: 4 (over y_lo, core), head: 8 (over x, y_hi), dp: 16 (over z).
Axes of the slice: x: 4, y: 4 (y_hi: 2, y_lo: 2; y = y_hi * 2 + y_lo), z: 16, core: 2. Of those that a mesh axis runs over, the one named last changes fastest.
Arguments:
- queries: bfloat16 [16, 2048, 4096], P('dp', 'seq', 'head'), may hold values from -2 to 2
- keys: bfloat16 [16, 2048, 4096], P('dp', 'seq', 'head'), may hold values from -2 to 2
- values: bfloat16 [16, 2048, 4096], P('dp', 'seq', 'head'), may hold values from -6 to 6
- out_proj: bfloat16 [4096, 1024], P('head', 'dp'), may hold values from -0.09375 to 0.09375
- depth_proj: bfloat16 [1024, 1024], P(None, ('head', 'dp')), may hold values from -0.1875 to 0.1875
- code_table: bfloat16 [2, 1024, 1024], P(None, ('head', 'dp')), may hold values from -6 to 6
- code_ids: int32 [16, 2048, 2], P('dp', ('seq', 'head')), may hold values from 0 to 1023
- depth_cotangent: bfloat16 [16, 2048, 2, 1024], P('dp', ('seq', 'head')), may hold values from -6 to 6
Outputs:
- grad_queries: bfloat16 [16, 2048, 4096], P('dp', 'seq', 'head')
- grad_keys: bfloat16 [16, 2048, 4096], P('dp', 'seq', 'head')
- grad_values: bfloat16 [16, 2048, 4096], P('dp', 'seq', 'head')
- grad_out_proj: float32 [4096, 1024], P('head', 'dp')
All inputs are finite; a program needn't handle non-finite values.
Results may differ from a plain program's by a relative error of at most 0.024.
Values may be sent and summed in bfloat16 or wider, within the bound.
A program may use at most 64 MiB of HBM per device.

v0:
```python
import jax
import jax.numpy as jnp
from jax import lax
from jax.sharding import PartitionSpec as P

DH = 128


def from_behind(block, axis, distance):
    devices = range(lax.axis_size(axis))
    route = [(i - distance, i) for i in devices if i - distance in devices]
    return lax.ppermute(block, axis, route)


def causal_mask(size):
    places = jnp.arange(size, dtype=jnp.int32)
    return (places[:, None] >= places[None, :]).astype(jnp.float32)


def depth_forward(carried, code_tab, proj_mat, code_rows):
    vocab_idx = jnp.arange(code_tab.shape[1], dtype=jnp.int32)
    level_outs = []
    for level_idx in range(code_tab.shape[0]):
        onehot = (code_rows[:, level_idx][:, None] == vocab_idx[None, :]).astype(jnp.bfloat16)
        embedded = jnp.dot(onehot, code_tab[level_idx], preferred_element_type=jnp.float32)
        summed = carried + embedded
        normed = (
            summed * lax.rsqrt(jnp.mean(summed * summed, axis=-1, keepdims=True) + 1e-05)
        ).astype(jnp.bfloat16)
        projected = jnp.dot(normed, proj_mat, preferred_element_type=jnp.float32)
        level_outs.append(projected)
        carried = summed + jax.nn.silu(projected)
    return jnp.stack(level_outs, axis=1)


def on_device(queries, keys, values, out_proj, depth_proj, code_table, code_ids, depth_cotangent):
    group_len = queries.shape[1]
    width_dev = queries.shape[2]
    heads_here = width_dev // DH
    att_scale = float(group_len * lax.axis_size("seq")) ** (-0.5)
    query_rows = queries[0].reshape(group_len, heads_here, DH)
    key_rows = keys[0].reshape(group_len, heads_here, DH)
    value_rows = values[0].reshape(group_len, heads_here, DH)
    causal = causal_mask(group_len)
    state_zero = jnp.zeros((heads_here, DH, DH), jnp.float32)
    state_local = jnp.einsum(
        "thd,the->hde", key_rows, value_rows, preferred_element_type=jnp.float32
    )
    state_acc = state_zero
    moving = state_local
    for hop_idx in range(lax.axis_size("seq") - 1):
        moving = from_behind(moving.astype(jnp.bfloat16), "seq", 1).astype(moving.dtype)
        state_acc = state_acc + moving
    state_in = state_acc.astype(jnp.bfloat16)
    scores = (
        jnp.einsum("thd,shd->hts", query_rows, key_rows, preferred_element_type=jnp.float32)
        * causal
    ).astype(jnp.bfloat16)
    attended = (
        att_scale
        * (
            jnp.einsum("hts,she->the", scores, value_rows, preferred_element_type=jnp.float32)
            + jnp.einsum("thd,hde->the", query_rows, state_in, preferred_element_type=jnp.float32)
        )
    ).astype(jnp.bfloat16)
    attended_flat = attended.reshape(group_len, width_dev)
    proj_full = lax.all_gather(out_proj, "dp", axis=1, tiled=True)
    mixed = lax.psum_scatter(
        jnp.dot(attended_flat, proj_full, preferred_element_type=jnp.float32).astype(jnp.bfloat16),
        "head",
        scatter_dimension=0,
        tiled=True,
    ).astype(jnp.float32)
    proj_mat, code_tab = (
        lax.all_gather(depth_proj, ("head", "dp"), axis=1, tiled=True),
        lax.all_gather(code_table, ("head", "dp"), axis=1, tiled=True),
    )
    code_rows = code_ids[0]
    cotangent = depth_cotangent[0].astype(jnp.float32)
    _, pullback = jax.vjp(
        lambda inputs: depth_forward(inputs, code_tab, proj_mat, code_rows), mixed
    )
    grad_mixed = pullback(cotangent)[0].astype(jnp.bfloat16)
    grad_block = lax.all_gather(grad_mixed, "head", axis=0, tiled=True)
    grad_att = lax.dot_general(
        grad_block, proj_full, (((1,), (1,)), ((), ())), preferred_element_type=jnp.float32
    )
    grad_rows = grad_att.astype(jnp.bfloat16).reshape(group_len, heads_here, DH)
    weight_term = lax.dot_general(
        attended_flat, grad_block, (((0,), (0,)), ((), ())), preferred_element_type=jnp.float32
    )
    weight_part = lax.psum_scatter(
        weight_term.astype(jnp.bfloat16), "dp", scatter_dimension=1, tiled=True
    )
    grad_out_proj = lax.psum(weight_part, "seq").astype(jnp.float32)
    back_local = jnp.einsum(
        "thd,the->hde", query_rows, grad_rows, preferred_element_type=jnp.float32
    )
    back_acc = state_zero
    moving_back = back_local
    for hop_idx in range(lax.axis_size("seq") - 1):
        moving_back = from_behind(moving_back.astype(jnp.bfloat16), "seq", -1).astype(
            moving_back.dtype
        )
        back_acc = back_acc + moving_back
    back_state = back_acc.astype(jnp.bfloat16)
    grad_scores = (
        jnp.einsum("the,she->hts", grad_rows, value_rows, preferred_element_type=jnp.float32)
        * causal
    ).astype(jnp.bfloat16)
    grad_query = att_scale * (
        jnp.einsum("hts,shd->thd", grad_scores, key_rows, preferred_element_type=jnp.float32)
        + jnp.einsum("the,hde->thd", grad_rows, state_in, preferred_element_type=jnp.float32)
    )
    grad_key = att_scale * (
        jnp.einsum("hts,thd->shd", grad_scores, query_rows, preferred_element_type=jnp.float32)
        + jnp.einsum("she,hde->shd", value_rows, back_state, preferred_element_type=jnp.float32)
    )
    grad_value = att_scale * (
        jnp.einsum("hts,the->she", scores, grad_rows, preferred_element_type=jnp.float32)
        + jnp.einsum("shd,hde->she", key_rows, back_state, preferred_element_type=jnp.float32)
    )
    out_shape = (1, group_len, width_dev)
    return (
        grad_query.reshape(out_shape).astype(jnp.bfloat16),
        grad_key.reshape(out_shape).astype(jnp.bfloat16),
        grad_value.reshape(out_shape).astype(jnp.bfloat16),
        grad_out_proj,
    )


def solution(mesh):
    in_specs = (
        P("dp", "seq", "head"),
        P("dp", "seq", "head"),
        P("dp", "seq", "head"),
        P("head", "dp"),
        P(None, ("head", "dp")),
        P(None, ("head", "dp"), None),
        P("dp", ("seq", "head"), None),
        P("dp", ("seq", "head"), None, None),
    )
    out_specs = (
        P("dp", "seq", "head"),
        P("dp", "seq", "head"),
        P("dp", "seq", "head"),
        P("head", "dp"),
    )
    return jax.shard_map(
        on_device, mesh=mesh, in_specs=in_specs, out_specs=out_specs, check_vma=False
    )
```

profile of v0, /device:TPU:1, one launch (start us, length us, event | category | flops | bytes accessed | tf_op | source)
XLA Modules:
  0.0 812.8 jit_solution(11603275540361019960)
XLA Ops:
  10.7 4.6 collective-permute-start
  16.4 3.3 collective-permute-done
  19.7 1.9 collective-permute-start.1
  21.6 2.0 multiply_convert_fusion.1
  23.6 4.2 collective-permute-start.2
  31.0 44.8 %all-gather.7.cloned.1.call-done = bf16[512,1024]{0,1:T(8,128)(2,1)} async-done(((bf16[512,64]{0,1:T(8,128)(2,1)}), bf16[512,1024]{0,1:T(8,128)(2,1)}) %all-gather.7.cloned.1.call-update) | async-done | bytes 1048592 | tf_op jit(solution)/shard_map/all_gather | solution.py:67
  75.7 3.2 convolution_convert_fusion.1
  81.3 210.8 %all-gather.5.cloned.1.call-done = bf16[1024,1024]{0,1:T(8,128)(2,1)} async-done(((bf16[1024,8]{0,1:T(8,128)(2,1)}), bf16[1024,1024]{0,1:T(8,128)(2,1)}) %all-gather.5.cloned.1.call-update) | async-done | bytes 2097168 | tf_op jit(solution)/shard_map/all_gather | solution.py:75
  292.2 2.1 fusion.16
  294.3 92.4 %reduce-scatter.3.cloned.1.call-done = bf16[64,1024]{1,0:T(8,128)(2,1)} async-done(((bf16[512,1024]{1,0:T(8,128)(2,1)}), bf16[64,1024]{1,0:T(8,128)(2,1)}) %reduce-scatter.3.cloned.1.call-update) | async-done | bytes 131088 | tf_op jit(solution)/shard_map/reduce_scatter | solution.py:68
  386.7 218.7 %all-gather.9.cloned.1.call-done = bf16[2,1024,1024]{2,1,0:T(8,128)(2,1)} async-done(((bf16[2,8,1024]{2,1,0:T(8,128)(2,1)}), bf16[2,1024,1024]{2,1,0:T(8,128)(2,1)}) %all-gather.9.cloned.1.call-update) | async-done | bytes 4194320 | tf_op jit(solution)/shard_map/all_gather | solution.py:76
  605.5 2.4 multiply_reduce_fusion.3
  608.6 2.3 multiply_reduce_fusion.2
  612.6 64.7 %all-gather.11.cloned.1.call-done = bf16[512,1024]{1,0:T(8,128)(2,1)} async-done(((bf16[64,1024]{1,0:T(8,128)(2,1)}), bf16[512,1024]{1,0:T(8,128)(2,1)}) %all-gather.11.cloned.1.call-update) | async-done | bytes 1048592 | tf_op jit(solution)/shard_map/all_gather | solution.py:84
  677.3 3.1 convolution_convert_fusion
  680.5 2.4 convolution_convert_fusion.2
  683.2 4.3 collective-permute-start.3
  690.3 1.9 collective-permute-start.4
  693.1 3.6 collective-permute-done.4
  696.7 1.9 collective-permute-start.5
  699.7 2.1 copy.29
  703.3 2.1 fusion.12
  705.4 36.8 %reduce-scatter.5.cloned.1.call-done = bf16[512,64]{0,1:T(8,128)(2,1)} async-done(((bf16[512,1024]{0,1:T(8,128)(2,1)}), bf16[512,64]{0,1:T(8,128)(2,1)}) %reduce-scatter.5.cloned.1.call-update) | async-done | bytes 65552 | tf_op jit(solution)/shard_map/reduce_scatter | solution.py:92
  745.6 58.9 %all-reduce.2.cloned.1.call-done = bf16[512,64]{0,1:T(8,128)(2,1)} async-done(((bf16[512,64]{0,1:T(8,128)(2,1)}), bf16[512,64]{0,1:T(8,128)(2,1)}) %all-reduce.2.cloned.1.call-update) | async-done | bytes 65552 | tf_op jit(solution)/shard_map/psum | solution.py:95
  (90 shorter events, 23.7 us)
Async XLA Ops:
  7.2 68.6 %all-gather.7.cloned.1.call-start = ((), (), s32[]{:S(2)}) async-start(), calls=%async_computation.3 | async-start | bytes 1114112 | tf_op jit(solution)/shard_map/all_gather | solution.py:67
  7.9 284.3 %all-gather.5.cloned.1.call-start = ((), (), s32[]{:S(2)}) async-start(), calls=%async_computation.2 | async-start | bytes 2113536 | tf_op jit(solution)/shard_map/all_gather | solution.py:75
  8.7 378.1 %reduce-scatter.3.cloned.1.call-start = ((), (), s32[]{:S(2)}) async-start(), calls=%async_computation.4 | async-start | bytes 1179648 | tf_op jit(solution)/shard_map/reduce_scatter | solution.py:68
  10.4 9.3 %copy-start.1 = (bf16[512,4,128]{2,1,0:T(4,128)(2,1)}, bf16[512,4,128]{2,1,0:T(4,128)(2,1)S(1)}, u32[]{:S(2)}) copy-start(bf16[512,4,128]{2,1,0:T(4,128)(2,1)S(1)} %reshape_squeeze.11) | copy-start | bytes 1572868
  10.7 9.0 %collective-permute-start = (bf16[4,128,128]{2,1,0:T(8,128)(2,1)S(1)}, bf16[4,128,128]{2,1,0:T(8,128)(2,1)S(1)}, u32[]{:S(2)}, u32[]{:S(2)}) collective-permute-start(bf16[4,128,128]{2,1,0:T(8,128)(2,1)S(1)} %convolution_convert_fusion.5), channel_id=1, source_target_pairs={{0,128},{128,256},{256,384},{1,129},{129,257},{257,385},{2,130},{1... | collective-permute-start | bytes 393224 | tf_op jit(solution)/shard_map/ppermute | solution.py:12
  19.7 3.9 collective-permute-start.1
  23.6 7.4 copy-start.14
  23.6 6.2 collective-permute-start.2
  29.8 49.2 %copy-start.16 = (bf16[4,128,128]{2,1,0:T(8,128)(2,1)}, bf16[4,128,128]{2,1,0:T(8,128)(2,1)S(1)}, u32[]{:S(2)}) copy-start(bf16[4,128,128]{2,1,0:T(8,128)(2,1)S(1)} %collective-permute-done.2) | copy-start | bytes 393220
  79.0 526.5 %all-gather.9.cloned.1.call-start = ((), (), s32[]{:S(2)}) async-start(), calls=%async_computation.5 | async-start | bytes 4227072 | tf_op jit(solution)/shard_map/all_gather | solution.py:76
  79.6 597.7 %all-gather.11.cloned.1.call-start = ((), (), s32[]{:S(2)}) async-start(), calls=%async_computation.6 | async-start | bytes 1179648 | tf_op jit(solution)/shard_map/all_gather | solution.py:84
  612.6 129.7 %reduce-scatter.5.cloned.1.call-start = ((), (), s32[]{:S(2)}) async-start(), calls=%async_computation.7 | async-start | bytes 1114112 | tf_op jit(solution)/shard_map/reduce_scatter | solution.py:92
  680.4 124.0 %all-reduce.2.cloned.1.call-start = ((), (), s32[]{:S(2)}) async-start(), calls=%async_computation.8 | async-start | bytes 131072 | tf_op jit(solution)/shard_map/psum | solution.py:95
  683.2 7.1 collective-permute-start.3
  690.2 8.4 %copy-start.15 = (bf16[4,128,128]{2,1,0:T(8,128)(2,1)S(1)}, bf16[4,128,128]{2,1,0:T(8,128)(2,1)}, u32[]{:S(2)}) copy-start(bf16[4,128,128]{2,1,0:T(8,128)(2,1)} %copy-done.14) | copy-start | bytes 393220
  690.2 8.4 %copy-start.17 = (bf16[4,128,128]{2,1,0:T(8,128)(2,1)S(1)}, bf16[4,128,128]{2,1,0:T(8,128)(2,1)}, u32[]{:S(2)}) copy-start(bf16[4,128,128]{2,1,0:T(8,128)(2,1)} %copy-done.16) | copy-start | bytes 393220
  690.3 9.4 %copy-start.18 = (bf16[4,128,128]{1,2,0:T(8,128)(2,1)}, bf16[4,128,128]{1,2,0:T(8,128)(2,1)S(1)}, u32[]{:S(2)}) copy-start(bf16[4,128,128]{1,2,0:T(8,128)(2,1)S(1)} %collective-permute-done.3) | copy-start | bytes 393220
  690.3 6.4 collective-permute-start.4
  693.1 10.2 %copy-start.8 = (bf16[512,4,128]{2,1,0:T(4,128)(2,1)S(1)}, bf16[512,4,128]{2,1,0:T(4,128)(2,1)}, u32[]{:S(2)}) copy-start(bf16[512,4,128]{2,1,0:T(4,128)(2,1)} %copy-done.7) | copy-start | bytes 1572868
  693.1 10.2 %copy-start.9 = (f32[4,128,512]{2,1,0:T(8,128)S(1)}, f32[4,128,512]{2,1,0:T(8,128)}, u32[]{:S(2)}) copy-start(f32[4,128,512]{2,1,0:T(8,128)} %fusion.45) | copy-start | bytes 3145732
  696.7 6.6 collective-permute-start.5
  699.7 42.5 %copy-start.4 = (bf16[512,4,128]{2,1,0:T(4,128)(2,1)S(1)}, bf16[512,4,128]{2,1,0:T(4,128)(2,1)}, u32[]{:S(2)}) copy-start(bf16[512,4,128]{2,1,0:T(4,128)(2,1)} %copy-done.1) | copy-start | bytes 1572868
  699.7 42.5 %copy-start.19 = (bf16[4,128,128]{1,2,0:T(8,128)(2,1)S(1)}, bf16[4,128,128]{1,2,0:T(8,128)(2,1)}, u32[]{:S(2)}) copy-start(bf16[4,128,128]{1,2,0:T(8,128)(2,1)} %copy-done.18) | copy-start | bytes 393220
  705.4 38.2 %copy-start.12 = (bf16[4,128,512]{2,1,0:T(8,128)(2,1)S(1)}, bf16[4,128,512]{2,1,0:T(8,128)(2,1)}, u32[]{:S(2)}) copy-start(bf16[4,128,512]{2,1,0:T(8,128)(2,1)} %fusion.12) | copy-start | bytes 1572868
  (12 other events, 53.7 us)
Sparse Core Ops, SparseCore 0:
  10.1 65.6 all-gather.6
  80.1 212.0 all-gather.4
  296.7 89.9 reduce-scatter.2
  391.0 214.4 all-gather.8
  612.7 64.5 all-gather.10
  680.6 61.6 reduce-scatter.4
  745.1 59.3 all-reduce.1
where the time goes:
time: 813 us
  waiting for transfers between devices  739 us (91%)
  matrix products  29.6 us (4%)
  starting transfers between devices  19.1 us (2%)
  between operations  14.6 us (2%)
  local copies, waits for them, and re-layouts  8.51 us (1%)
    all_gather x1, waiting for transfers between devices, on_device(): lax.all_gather(code_table, ('head', 'dp'), axis=1, tiled=True)  219 us
    all_gather x1, waiting for transfers between devices, on_device(): lax.all_gather(depth_proj, ('head', 'dp'), axis=1, tiled=True)  211 us
    reduce_scatter x1, waiting for transfers between devices, on_device(): lax.psum_scatter(jnp.dot(attended_flat, proj_full, preferred_element_type...  92.4 us
    all_gather x1, waiting for transfers between devices, on_device(): grad_block = lax.all_gather(grad_mixed, 'head', axis=0, tiled=True)  64.7 us
    psum x1, waiting for transfers between devices, on_device(): grad_out_proj = lax.psum(weight_part, 'seq').astype(jnp.float32)  58.9 us
    all_gather x1, waiting for transfers between devices, on_device(): proj_full = lax.all_gather(out_proj, 'dp', axis=1, tiled=True)  44.8 us
    reduce_scatter x1, waiting for transfers between devices, on_device(): lax.psum_scatter(weight_term.astype(jnp.bfloat16), 'dp', scatter_dimensio...  36.8 us
    ppermute x6, starting transfers between devices, from_behind(): return lax.ppermute(block, axis, route)  18.9 us
  transfers between devices with their start and end apart: 13, of which 12 were waited for; matrix products, arithmetic and copies ran while one was open for 4% of the time, Pallas kernels for 0%

commit v1 on v0

v1 whole, which is shorter than its diff:
```python
import functools

import jax
import jax.numpy as jnp
from jax import lax
from jax.experimental import pallas as pl
from jax.experimental.pallas import tpu as pltpu
from jax.sharding import PartitionSpec as P

DH = 128
F32 = jnp.float32
BF16 = jnp.bfloat16
EPS = 1e-05
HALF = 256
N_COPIES = 200


def dot(a, b):
    return lax.dot_general(a, b, (((1,), (0,)), ((), ())), preferred_element_type=F32)


def dot_nt(a, b):
    return lax.dot_general(a, b, (((1,), (1,)), ((), ())), preferred_element_type=F32)


def dot_tn(a, b):
    return lax.dot_general(a, b, (((0,), (0,)), ((), ())), preferred_element_type=F32)


class Copies:
    def __init__(self, send_sems, recv_sems):
        self.send_sems, self.recv_sems, self.all = send_sems, recv_sems, []

    def send(self, src, dst, device):
        index = len(self.all)
        copy = pltpu.make_async_remote_copy(
            src_ref=src,
            dst_ref=dst,
            send_sem=self.send_sems.at[index],
            recv_sem=self.recv_sems.at[index],
            device_id=device,
            device_id_type=pl.DeviceIdType.MESH,
        )
        copy.start()
        self.all.append(copy)
        return copy

    def drain(self):
        for copy in self.all:
            copy.wait_send()


def kernel(
    scale,
    q_ref, k_ref, v_ref, op_ref, wp_ref, ids_ref, cot_ref,
    gq_ref, gk_ref, gv_ref, go_ref,
    wz, proj, wts,
    s_own, s_recv, t_own, t_recv, s_in,
    b_own, b_recv, bt_own, bt_recv, b_in,
    sc, acc, att,
    mix, ra1, rb1, ra2, rb2, ray, rar, raf, rbr, rbf, yb, sb1, sb2,
    mixed, emb, gpre,
    gb, gra, grb,
    ga, wg, wgr, zsend_r, zrecv_r, zsend_l, zrecv_l, y_own, y_recv, o_own, o_recv,
    send_sems, recv_sems,
):
    seq, head, z = lax.axis_index("seq"), lax.axis_index("head"), lax.axis_index("dp")
    x, yh, yl, c = head // 2, head % 2, seq // 2, seq % 2
    y = 2 * yh + yl
    nz = 16

    def at_x(step):
        return (x + step + 4) % 4

    def at_y(step):
        return (y + step + 4) % 4

    def at_z(step):
        return (z + step + nz) % nz

    def dev(x_=None, y_=None, z_=None, c_=None):
        x_ = x if x_ is None else x_
        y_ = y if y_ is None else y_
        z_ = z if z_ is None else z_
        c_ = c if c_ is None else c_
        return {"seq": 2 * (y_ % 2) + c_, "head": 2 * x_ + y_ // 2, "dp": z_}

    xp, xm = dev(x_=at_x(1)), dev(x_=at_x(-1))
    yp, ym = dev(y_=at_y(1)), dev(y_=at_y(-1))
    zp, zm = dev(z_=at_z(1)), dev(z_=at_z(-1))
    mate = dev(c_=1 - c)
    pair = dev(y_=2 * yh + 1 - yl)
    cf, ylf = c.astype(F32), yl.astype(F32)
    go = Copies(send_sems, recv_sems)

    barrier = pltpu.get_barrier_semaphore()
    for other in (xp, xm, yp, ym, zp, zm, mate):
        pl.semaphore_signal(barrier, inc=1, device_id=other, device_id_type=pl.DeviceIdType.MESH)

    def hs(i):
        return slice(i * DH, (i + 1) * DH)

    for i in range(4):
        s_own[i] = dot_tn(k_ref[:, hs(i)], v_ref[:, hs(i)]).astype(BF16)
    pl.semaphore_wait(barrier, 7)

    quarter = 2 * c + yl
    mine = c * 32

    state_copy = go.send(s_own, s_recv, mate)
    own_w = wp_ref.at[quarter]
    own_p = op_ref.at[pl.ds(pl.multiple_of(mine, 32), 32), :]

    def w_slot(j):
        return wz.at[j]

    def p_slot(j):
        return proj.at[j, c]

    wr = go.send(own_w, w_slot(z), zp)
    wl = go.send(own_w, w_slot(z), zm)
    pr = go.send(own_p, p_slot(z), zp)
    pll = go.send(own_p, p_slot(z), zm)
    wz[z] = wp_ref[quarter]
    proj[z] = op_ref[...].reshape(2, 32, 512)

    rows = lax.broadcasted_iota(jnp.int32, (HALF, HALF), 0)
    cols = lax.broadcasted_iota(jnp.int32, (HALF, HALF), 1)
    low = rows >= cols
    top, bot = slice(0, HALF), slice(HALF, 2 * HALF)

    def scores_of(a_ref, b_ref, i):
        a0, a1 = a_ref[top, hs(i)], a_ref[bot, hs(i)]
        b0, b1 = b_ref[top, hs(i)], b_ref[bot, hs(i)]
        m00 = jnp.where(low, dot_nt(a0, b0), 0.0).astype(BF16)
        m10 = dot_nt(a1, b0).astype(BF16)
        m11 = jnp.where(low, dot_nt(a1, b1), 0.0).astype(BF16)
        return m00, m10, m11

    def forward(i):
        m00, m10, m11 = scores_of(q_ref, k_ref, i)
        sc[i, 0], sc[i, 1], sc[i, 2] = m00, m10, m11
        v0, v1 = v_ref[top, hs(i)], v_ref[bot, hs(i)]
        acc[top, hs(i)] = dot(m00, v0)
        acc[bot, hs(i)] = dot(m10, v0) + dot(m11, v1)

    def pass_state():
        state_copy.wait_recv()
        t_own[...] = (s_own[...].astype(F32) + s_recv[...].astype(F32)).astype(BF16)
        return go.send(t_own, t_recv, pair)

    def finish_attended():
        pair_copy.wait_recv()
        s_in[...] = (cf * s_recv[...].astype(F32) + ylf * t_recv[...].astype(F32)).astype(BF16)
        for i in range(4):
            att[:, hs(i)] = (
                scale * (acc[:, hs(i)] + dot(q_ref[:, hs(i)], s_in[i]))
            ).astype(BF16)

    pair_copy = None
    to_mate = []
    for step in range(1, 9):
        wr.wait_recv()
        if step < 8:
            src = at_z(-step)
            wr = go.send(w_slot(src), w_slot(src), zp)
            wl.wait_recv()
        if step < 7:
            src = at_z(step)
            wl = go.send(w_slot(src), w_slot(src), zm)
        pr.wait_recv()
        src = at_z(-step)
        if step < 8:
            pr = go.send(p_slot(src), p_slot(src), zp)
        to_mate.append(go.send(p_slot(src), p_slot(src), mate))
        if step < 8:
            pll.wait_recv()
            src = at_z(step)
            if step < 7:
                pll = go.send(p_slot(src), p_slot(src), zm)
            to_mate.append(go.send(p_slot(src), p_slot(src), mate))
        if step == 1:
            pair_copy = pass_state()
        if step <= 4:
            forward(step - 1)
        if step == 5:
            finish_attended()

    q0 = pl.multiple_of(quarter * 256, 256)
    c0 = pl.multiple_of(c * 512, 512)
    for a in range(3):
        for hf in range(2):
            block = wz[hf * 8:hf * 8 + 8, a].astype(F32)
            piece = jnp.concatenate(
                [block[:, :8].reshape(64, 128), block[:, 8:].reshape(64, 128)], axis=1
            )
            wts[a, x, yh, hf, :, pl.ds(q0, 256)] = piece.astype(BF16)

    def qcols(y_):
        return pl.ds(pl.multiple_of((2 * c + y_ % 2) * 256, 256), 256)

    ccols = pl.ds(c0, 512)

    def send_w(win, device):
        return go.send(win, win, device)

    def wa_x(xx, r0=0, n=64):
        return wts.at[:, xx, yh, 0, pl.ds(r0, n), qcols(y)]

    def wb_y(yy, r0=0, n=64):
        return wts.at[:, x, yy // 2, 1, pl.ds(r0, n), qcols(yy)]

    def wa_y(a, yy, r0=0, n=64):
        return wts.at[a, :, yy // 2, 0, pl.ds(r0, n), qcols(yy)]

    def wb_x(a, xx, r0=0, n=64):
        return wts.at[a, xx, :, 1, pl.ds(r0, n), ccols]

    wax_p, wax_m = send_w(wa_x(x), xp), send_w(wa_x(x), xm)
    wby_p, wby_m = send_w(wb_y(y), yp), send_w(wb_y(y), ym)

    for copy in to_mate:
        copy.wait_recv()

    def mix_block(j):
        part = dot_nt(att[...], proj[4 * j:4 * j + 4].reshape(256, 512))
        mix[:, :, :, :, 256 * j:256 * j + 256] = part.astype(BF16).reshape(4, 2, 2, 32, 256)

    al, be = slice(0, 512), slice(512, 1024)
    mix_block(2)
    mix_block(3)
    mby_p = go.send(mix.at[:, 1 - yh, 0, :, pl.ds(512, 512)], rbr.at[0], yp)
    mby_m = go.send(mix.at[:, 1 - yh, 1, :, pl.ds(512, 512)], rbr.at[1], ym)
    mix_block(0)
    mix_block(1)
    max_p = go.send(mix.at[at_x(2), 0, :, :, pl.ds(0, 512)], ra1, xp)
    max_m = go.send(mix.at[at_x(2), 1, :, :, pl.ds(0, 512)], rb1, xm)

    wax_p.wait_recv()
    wax_m.wait_recv()
    wax2_p = send_w(wa_x(at_x(-1), 0, 32), xp)
    wax2_m = send_w(wa_x(at_x(1), 32, 32), xm)
    wby_p.wait_recv()
    wby_m.wait_recv()
    wby2_p = send_w(wb_y(at_y(-1), 0, 32), yp)
    wby2_m = send_w(wb_y(at_y(1), 32, 32), ym)

    mby_p.wait_recv()
    mby_m.wait_recv()
    mbf_p = go.send(rbr.at[0], rbf.at[0], yp)
    mbf_m = go.send(rbr.at[1], rbf.at[1], ym)
    max_p.wait_recv()
    max_m.wait_recv()
    mix[at_x(1), 0, :, :, al] = (
        mix[at_x(1), 0, :, :, al].astype(F32) + ra1[...].astype(F32)
    ).astype(BF16)
    mix[at_x(-1), 1, :, :, al] = (
        mix[at_x(-1), 1, :, :, al].astype(F32) + rb1[...].astype(F32)
    ).astype(BF16)
    max2_p = go.send(mix.at[at_x(1), :, :, :, pl.ds(0, 512)], ra2, xp)
    max2_m = go.send(mix.at[at_x(-1), :, :, :, pl.ds(0, 512)], rb2, xm)

    wax2_p.wait_recv()
    wax2_m.wait_recv()
    wby2_p.wait_recv()
    wby2_m.wait_recv()
    way, wbx = [None] * 3, [None] * 3
    w_mate = []

    def bulk(a):
        way[a] = (send_w(wa_y(a, y), yp), send_w(wa_y(a, y), ym))
        wbx[a] = (send_w(wb_x(a, x), xp), send_w(wb_x(a, x), xm))
        w_mate.append(send_w(wa_y(a, y), mate))
        w_mate.append(send_w(wb_x(a, x), mate))

    way2, wbx2 = [None] * 3, [None] * 3

    def bulk_relay(a):
        for copy in way[a] + wbx[a]:
            copy.wait_recv()
        way2[a] = (
            send_w(wa_y(a, at_y(-1), 0, 32), yp),
            send_w(wa_y(a, at_y(1), 32, 32), ym),
        )
        wbx2[a] = (
            send_w(wb_x(a, at_x(-1), 0, 32), xp),
            send_w(wb_x(a, at_x(1), 32, 32), xm),
        )
        w_mate.append(send_w(wa_y(a, at_y(-1)), mate))
        w_mate.append(send_w(wa_y(a, at_y(1)), mate))
        w_mate.append(send_w(wb_x(a, at_x(-1)), mate))
        w_mate.append(send_w(wb_x(a, at_x(1)), mate))

    def bulk_end(a):
        for copy in way2[a] + wbx2[a]:
            copy.wait_recv()
        w_mate.append(send_w(wa_y(a, at_y(2)), mate))
        w_mate.append(send_w(wb_x(a, at_x(2)), mate))

    bulk(1)
    mbf_p.wait_recv()
    mbf_m.wait_recv()
    for hf in range(2):
        yb[:, hf] = (
            mix[:, yh, hf, :, be].astype(F32) + rbf[hf].astype(F32)
        ).astype(BF16)
    mbx_p = go.send(yb.at[at_x(2), 0], sb1.at[0], xp)
    mbx_m = go.send(yb.at[at_x(2), 1], sb1.at[1], xm)
    max2_p.wait_recv()
    max2_m.wait_recv()
    ray[...] = (
        mix[x, 1 - yh, :, :, al].astype(F32)
        + ra2[1 - yh].astype(F32)
        + rb2[1 - yh].astype(F32)
    ).astype(BF16)
    may_p = go.send(ray.at[0], rar.at[0], yp)
    may_m = go.send(ray.at[1], rar.at[1], ym)
    mixed[:, al] = (
        mix[x, yh, :, :, al].astype(F32) + ra2[yh].astype(F32) + rb2[yh].astype(F32)
    ).reshape(64, 512)
    bulk(0)
    mbx_p.wait_recv()
    mbx_m.wait_recv()
    yb[at_x(1), 0] = (yb[at_x(1), 0].astype(F32) + sb1[0].astype(F32)).astype(BF16)
    yb[at_x(-1), 1] = (yb[at_x(-1), 1].astype(F32) + sb1[1].astype(F32)).astype(BF16)
    mbx2_p = go.send(yb.at[at_x(1)], sb2.at[0], xp)
    mbx2_m = go.send(yb.at[at_x(-1)], sb2.at[1], xm)
    may_p.wait_recv()
    may_m.wait_recv()
    maf_p = go.send(rar.at[0], raf.at[0], yp)
    maf_m = go.send(rar.at[1], raf.at[1], ym)
    bulk(2)
    bulk_relay(1)
    maf_p.wait_recv()
    maf_m.wait_recv()
    mixed[:, al] = mixed[:, al] + raf[...].astype(F32).reshape(64, 512)
    mbx2_p.wait_recv()
    mbx2_m.wait_recv()
    mixed[:, be] = (
        yb[x].astype(F32) + sb2[0].astype(F32) + sb2[1].astype(F32)
    ).reshape(64, 512)
    bulk_relay(0)
    bulk_end(1)
    bulk_relay(2)
    bulk_end(0)
    bulk_end(2)
    for copy in w_mate:
        copy.wait_recv()

    def weight(a, xx):
        return wts[a, xx].reshape(256, 1024)

    vocab = lax.broadcasted_iota(jnp.int32, (64, 1024), 1)
    for level in range(2):
        onehot = jnp.where(ids_ref[:, level:level + 1] == vocab, 1.0, 0.0).astype(BF16)
        total = None
        for xx in range(4):
            term = dot(onehot[:, 256 * xx:256 * xx + 256], weight(1 + level, xx))
            total = term if total is None else total + term
        emb[level] = total

    def back_through(g):
        total = None
        for xx in range(4):
            term = dot(g[:, 256 * xx:256 * xx + 256], weight(0, xx))
            total = term if total is None else total + term
        return total

    gpre[...] = back_through(cot_ref[1])

    def mean_of(value):
        return jnp.mean(value, axis=-1, keepdims=True)

    summed1 = mixed[...] + emb[0]
    r1 = lax.rsqrt(mean_of(summed1 * summed1) + EPS)
    normed1 = (summed1 * r1).astype(BF16)
    mixed[...] = summed1
    proj1 = jnp.concatenate([dot_nt(normed1, weight(0, xx)) for xx in range(4)], axis=1)
    sig = jax.nn.sigmoid(proj1)
    summed2 = summed1 + proj1 * sig + emb[1]
    r2 = lax.rsqrt(mean_of(summed2 * summed2) + EPS)
    g2 = gpre[...]
    gsum = r2 * g2 - summed2 * (r2 * r2 * r2 * mean_of(g2 * summed2))
    emb[0] = gsum
    gproj = cot_ref[0].astype(F32) + gsum * (sig * (1.0 + proj1 * (1.0 - sig)))
    g1 = back_through(gproj.astype(BF16))
    summed1 = mixed[...]
    grad = emb[0] + r1 * g1 - summed1 * (r1 * r1 * r1 * mean_of(g1 * summed1))
    gb[x, yh] = grad.astype(BF16).reshape(2, 32, 1024)

    cal, cbe = pl.ds(0, 512), pl.ds(512, 512)

    def same(win, device):
        return go.send(win, win, device)

    def pieces(*idx):
        return gb.at[idx]

    bx1_p = go.send(pieces(x, yh, 0, slice(None), cbe), grb.at[0], yp)
    bx1_m = go.send(pieces(x, yh, 1, slice(None), cbe), grb.at[1], ym)
    own_a = gb.at[x, yh, :, :, cal]
    ax_p, ax_m = same(own_a, xp), same(own_a, xm)
    bx1_p.wait_recv()
    bx1_m.wait_recv()
    b2_p = go.send(grb.at[0], gb.at[x, at_y(-1) // 2, 0, :, cbe], yp)
    b2_m = go.send(grb.at[1], gb.at[x, at_y(1) // 2, 1, :, cbe], ym)
    ax_p.wait_recv()
    ax_m.wait_recv()
    ax2_p = same(gb.at[at_x(-1), yh, 0, :, cal], xp)
    ax2_m = same(gb.at[at_x(1), yh, 1, :, cal], xm)
    b2_p.wait_recv()
    b2_m.wait_recv()
    own_b = gb.at[x, :, :, :, cbe]
    bx_p, bx_m = same(own_b, xp), same(own_b, xm)
    ax2_p.wait_recv()
    ax2_m.wait_recv()
    ay_p = go.send(gb.at[:, yh, 0, :, cal], gra.at[0], yp)
    ay_m = go.send(gb.at[:, yh, 1, :, cal], gra.at[1], ym)
    bx_p.wait_recv()
    bx_m.wait_recv()
    bx2_p = same(gb.at[at_x(-1), 0, :, :, cbe], xp)
    bx2_m = same(gb.at[at_x(1), 1, :, :, cbe], xm)
    ay_p.wait_recv()
    ay_m.wait_recv()
    af_p = go.send(gra.at[0], gb.at[:, at_y(-1) // 2, 0, :, cal], yp)
    af_m = go.send(gra.at[1], gb.at[:, at_y(1) // 2, 1, :, cal], ym)

    def weight_grad(j):
        block = gb[:, :, :, :, 256 * j:256 * j + 256].reshape(512, 256)
        wg[4 * j:4 * j + 4] = dot_tn(block, att[...]).astype(BF16).reshape(4, 2, 32, 512)

    bx2_p.wait_recv()
    bx2_m.wait_recv()
    weight_grad(2)
    weight_grad(3)
    wg_b = go.send(wg.at[pl.ds(8, 8), 1 - c], wgr.at[pl.ds(8, 8)], mate)
    af_p.wait_recv()
    af_m.wait_recv()
    weight_grad(0)
    weight_grad(1)
    wg_a = go.send(wg.at[pl.ds(0, 8), 1 - c], wgr.at[pl.ds(0, 8)], mate)

    for j in range(2):
        total = None
        for zz in range(4):
            term = dot(
                gb[:, :, :, :, 256 * zz:256 * zz + 256].reshape(512, 256),
                proj[4 * zz:4 * zz + 4, :, :, 256 * j:256 * j + 256].reshape(256, 256),
            )
            total = term if total is None else total + term
        ga[:, 256 * j:256 * j + 256] = total.astype(BF16)

    for i in range(4):
        b_own[i] = dot_tn(q_ref[:, hs(i)], ga[:, hs(i)]).astype(BF16)
    back_copy = go.send(b_own, b_recv, mate)
    wg_b.wait_recv()
    wg_a.wait_recv()

    def own_chunk(j):
        return wg[j, c].astype(F32) + wgr[j].astype(F32)

    def ring_step(step, last_r, last_l):
        if step <= 7:
            value = own_chunk(at_z(8 - step))
            if last_r is not None:
                last_r.wait_recv()
                value = value + zrecv_r[step - 2].astype(F32)
            zsend_r[step - 1] = value.astype(BF16)
            last_r = go.send(zsend_r.at[step - 1], zrecv_r.at[step - 1], zp)
        value = own_chunk(at_z(step - 9))
        if last_l is not None:
            last_l.wait_recv()
            value = value + zrecv_l[step - 2].astype(F32)
        zsend_l[step - 1] = value.astype(BF16)
        last_l = go.send(zsend_l.at[step - 1], zrecv_l.at[step - 1], zm)
        return last_r, last_l

    def backward(i):
        q0_, q1_ = q_ref[top, hs(i)], q_ref[bot, hs(i)]
        k0_, k1_ = k_ref[top, hs(i)], k_ref[bot, hs(i)]
        v0_, v1_ = v_ref[top, hs(i)], v_ref[bot, hs(i)]
        a0_, a1_ = ga[top, hs(i)], ga[bot, hs(i)]
        m00, m10, m11 = scores_of(ga, v_ref, i)
        e, b = s_in[i], b_in[i]
        gq_ref[top, hs(i)] = (scale * (dot(m00, k0_) + dot_nt(a0_, e))).astype(BF16)
        gq_ref[bot, hs(i)] = (
            scale * (dot(m10, k0_) + dot(m11, k1_) + dot_nt(a1_, e))
        ).astype(BF16)
        gk_ref[top, hs(i)] = (
            scale * (dot_tn(m00, q0_) + dot_tn(m10, q1_) + dot_nt(v0_, b))
        ).astype(BF16)
        gk_ref[bot, hs(i)] = (scale * (dot_tn(m11, q1_) + dot_nt(v1_, b))).astype(BF16)
        gv_ref[top, hs(i)] = (
            scale * (dot_tn(sc[i, 0], a0_) + dot_tn(sc[i, 1], a1_) + dot(k0_, b))
        ).astype(BF16)
        gv_ref[bot, hs(i)] = (scale * (dot_tn(sc[i, 2], a1_) + dot(k1_, b))).astype(BF16)

    last_r, last_l = ring_step(1, None, None)
    back_copy.wait_recv()
    bt_own[...] = (b_own[...].astype(F32) + b_recv[...].astype(F32)).astype(BF16)
    back_pair = go.send(bt_own, bt_recv, pair)
    for step in range(2, 9):
        last_r, last_l = ring_step(step, last_r if step <= 7 else last_r, last_l)
        if step == 3:
            back_pair.wait_recv()
            b_in[...] = (
                (1.0 - cf) * b_recv[...].astype(F32) + (1.0 - ylf) * bt_recv[...].astype(F32)
            ).astype(BF16)
        if 3 <= step <= 6:
            backward(step - 3)
    last_r.wait_recv()
    last_l.wait_recv()
    y_own[...] = (
        own_chunk(z) + zrecv_r[6].astype(F32) + zrecv_l[7].astype(F32)
    ).astype(BF16)
    y_copy = go.send(y_own, y_recv, pair)
    y_copy.wait_recv()
    o_own[...] = y_own[...].astype(F32) + y_recv[...].astype(F32)
    o_copy = go.send(o_own, o_recv, mate)
    go_ref[pl.ds(pl.multiple_of(mine, 32), 32), :] = o_own[...]
    o_copy.wait_recv()
    go_ref[pl.ds(pl.multiple_of(32 - mine, 32), 32), :] = o_recv[...]
    go.drain()


def on_device(queries, keys, values, out_proj, depth_proj, code_table, code_ids, depth_cotangent):
    scale = 2048.0 ** (-0.5)
    stacked = jnp.concatenate([depth_proj.T[None], code_table], axis=0)
    packed = (
        stacked.reshape(3, 8, 4, 2, 128).transpose(2, 0, 3, 1, 4).reshape(4, 3, 16, 128)
    )
    cot = jnp.transpose(depth_cotangent[0], (1, 0, 2))

    def vm(shape, kind=BF16):
        return pltpu.VMEM(shape, kind)

    state = vm((4, DH, DH))
    gq, gk, gv, gop = pl.pallas_call(
        functools.partial(kernel, scale),
        out_shape=(
            jax.ShapeDtypeStruct((512, 512), BF16),
            jax.ShapeDtypeStruct((512, 512), BF16),
            jax.ShapeDtypeStruct((512, 512), BF16),
            jax.ShapeDtypeStruct((64, 512), F32),
        ),
        in_specs=[pl.BlockSpec(memory_space=pltpu.VMEM)] * 7,
        out_specs=(pl.BlockSpec(memory_space=pltpu.VMEM),) * 4,
        scratch_shapes=[
            vm((16, 3, 16, 128)), vm((16, 2, 32, 512)), vm((3, 4, 2, 2, 64, 1024)),
            state, state, state, state, state,
            state, state, state, state, state,
            vm((4, 3, 256, 256)), vm((512, 512), F32), vm((512, 512)),
            vm((4, 2, 2, 32, 1024)),
            vm((2, 32, 512)), vm((2, 32, 512)),
            vm((2, 2, 32, 512)), vm((2, 2, 32, 512)),
            vm((2, 32, 512)), vm((2, 32, 512)), vm((2, 32, 512)),
            vm((2, 4, 32, 512)), vm((2, 4, 32, 512)),
            vm((4, 2, 32, 512)), vm((2, 32, 512)), vm((2, 2, 32, 512)),
            vm((64, 1024), F32), vm((2, 64, 1024), F32), vm((64, 1024), F32),
            vm((4, 2, 2, 32, 1024)), vm((2, 4, 32, 512)), vm((2, 32, 512)),
            vm((512, 512)), vm((16, 2, 32, 512)), vm((16, 32, 512)),
            vm((7, 32, 512)), vm((7, 32, 512)), vm((8, 32, 512)), vm((8, 32, 512)),
            vm((32, 512)), vm((32, 512)), vm((32, 512), F32), vm((32, 512), F32),
            pltpu.SemaphoreType.DMA((N_COPIES,)),
            pltpu.SemaphoreType.DMA((N_COPIES,)),
        ],
        compiler_params=pltpu.CompilerParams(
            collective_id=0, has_side_effects=True, vmem_limit_bytes=60 * 1024 * 1024
        ),
        name="fused_step",
    )(
        queries[0], keys[0], values[0], out_proj.T, packed, code_ids[0], cot,
    )
    return gq[None], gk[None], gv[None], gop.T


def solution(mesh):
    in_specs = (
        P("dp", "seq", "head"),
        P("dp", "seq", "head"),
        P("dp", "seq", "head"),
        P("head", "dp"),
        P(None, ("head", "dp")),
        P(None, ("head", "dp"), None),
        P("dp", ("seq", "head"), None),
        P("dp", ("seq", "head"), None, None),
    )
    out_specs = (
        P("dp", "seq", "head"),
        P("dp", "seq", "head"),
        P("dp", "seq", "head"),
        P("head", "dp"),
    )
    return jax.shard_map(
        on_device, mesh=mesh, in_specs=in_specs, out_specs=out_specs, check_vma=False
    )
```

time: 813 us -> 135 us (0.17)
  waiting for transfers between devices: 739 us -> 0 us
  Pallas kernels: 0 us -> 125 us
  matrix products: 29.6 us -> 0 us
  starting transfers between devices: 19.1 us -> 0 us
  between operations: 14.6 us -> 0.66 us
    all_gather x4 -> x0, waiting for transfers between devices: 539 us -> none  [the longest x1 219 us: on_device(): lax.all_gather(code_table, ('head', 'dp'), axis=1, tiled=True)]
    reduce_scatter x2 -> x0, waiting for transfers between devices: 129 us -> none  [the longest x1 92.4 us: on_device(): lax.psum_scatter(jnp.dot(attended_flat, proj_full, preferred_element_type...]
    pallas_call x0 -> x1, Pallas kernels: none -> 125 us  [on_device(): pl.pallas_call(functools.partial(kernel, scale), out_shape=(jax.ShapeDtyp...]
    psum x1 -> x0, waiting for transfers between devices: 58.9 us -> none  [on_device(): grad_out_proj = lax.psum(weight_part, 'seq').astype(jnp.float32)]
    dot_general x20 -> x0, matrix products: 29.6 us -> none  [the longest x2 4.69 us: depth_forward(): jnp.dot(onehot, code_tab[level_idx], preferred_element_type=jnp.float32)]
    ppermute x6 -> x0, starting transfers between devices: 18.9 us -> none  [from_behind(): return lax.ppermute(block, axis, route)]
    ppermute x6 -> x0, waiting for transfers between devices: 9.56 us -> none  [from_behind(): return lax.ppermute(block, axis, route)]
  transfers between devices with their start and end apart: 13 -> 0, of which waited for: 12 -> 0; matrix products, arithmetic and copies ran while one was open for 4% -> 0% of each run, Pallas kernels for 0% -> 0%
where the time goes in v1:
time: 135 us
  Pallas kernels  125 us (93%)
  local copies, waits for them, and re-layouts  7.93 us (6%)
    pallas_call x1, Pallas kernels, on_device(): pl.pallas_call(functools.partial(kernel, scale), out_shape=(jax.ShapeDtyp...  125 us
    unnamed x13, local copies, waits for them, and re-layouts  6.54 us

profile of v1, /device:TPU:1, one launch (start us, length us, event | category | flops | bytes accessed | tf_op | source)
XLA Modules:
  0.0 134.9 jit_solution(506994959192208901)
XLA Ops:
  0.6 0.0 copy-start.3
  0.6 1.4 %copy.15.ids_ref = s32[64,2]{1,0:T(8,128)} copy(s32[64,2]{0,1:T(2,128)} %bitcast.35) | data formatting | bytes 1024 | tf_op jit(solution)/shard_map/squeeze | solution.py:572
  2.0 0.0 copy-done.3
  2.0 1.3 maximum_bitcast_fusion.wp_ref
  3.4 1.7 %copy.19 = bf16[1,64,2,1024]{3,1,2,0:T(8,128)(2,1)} copy(bf16[1,64,2,1024]{3,2,1,0:T(2,128)(2,1)} %param.15) | data formatting | bytes 524288 | tf_op args[7]
  5.1 125.0 %fused_step.1 = (bf16[512,512]{1,0:T(8,128)(2,1)}, bf16[512,512]{1,0:T(8,128)(2,1)}, bf16[512,512]{1,0:T(8,128)(2,1)}, f32[64,512]{1,0:T(8,128)}) custom-call(bf16[512,512]{1,0:T(8,128)(2,1)} %bitcast.28, bf16[512,512]{1,0:T(8,128)(2,1)} %bitcast.29, bf16[512,512]{1,0:T(8,128)(2,1)} %bitcast.30, bf16[64,512]{1,0:T(8,128)(2,1)} %bitcast.32, ...), custom_call_target="tpu_custom_call" | custom-call | tf_op jit(solution)/shard_map/fused_step/pallas_call | solution.py:538
  130.1 0.0 copy-start.1
  130.1 1.9 %copy.24 = bf16[1,512,512]{2,1,0:T(8,128)(2,1)} copy(bf16[1,512,512]{2,1,0:T(8,128)(2,1)} %bitcast.27) | data formatting | bytes 1048576
  132.0 0.0 copy-done.1
  132.0 0.0 copy-start
  132.0 0.8 copy.25
  132.8 0.4 copy-done
  133.3 0.0 copy-start.2
  133.3 0.8 copy.26
  134.1 0.2 copy-done.2
  134.3 0.7 copy.27
Async XLA Ops:
  0.6 1.4 %copy-start.3 = (bf16[2,8,1024]{2,1,0:T(8,128)(2,1)S(1)}, bf16[2,8,1024]{2,1,0:T(8,128)(2,1)}, u32[]{:S(2)}) copy-start(bf16[2,8,1024]{2,1,0:T(8,128)(2,1)} %param.13) | copy-start | bytes 98308
  130.1 1.9 %copy-start.1 = (bf16[512,512]{1,0:T(8,128)(2,1)S(1)}, bf16[512,512]{1,0:T(8,128)(2,1)}, u32[]{:S(2)}) copy-start(bf16[512,512]{1,0:T(8,128)(2,1)} %get-tuple-element.9) | copy-start | bytes 1572868
  132.0 1.2 copy-start
  133.3 1.0 copy-start.2

commit v2 on v1

--- a/solution.py
+++ b/solution.py
@@ -12,7 +12,7 @@
 BF16 = jnp.bfloat16
 EPS = 1e-05
 HALF = 256
-N_COPIES = 200
+N_COPIES = 256
 
 
 def dot(a, b):
@@ -52,7 +52,7 @@
 
 def kernel(
     scale,
-    q_ref, k_ref, v_ref, op_ref, wp_ref, ids_ref, cot_ref,
+    q_ref, k_ref, v_ref, op_ref, dp_ref, tab_ref, ids_ref, cot_ref,
     gq_ref, gk_ref, gv_ref, go_ref,
     wz, proj, wts,
     s_own, s_recv, t_own, t_recv, s_in,
@@ -61,7 +61,7 @@
     mix, ra1, rb1, ra2, rb2, ray, rar, raf, rbr, rbf, yb, sb1, sb2,
     mixed, emb, gpre,
     gb, gra, grb,
-    ga, wg, wgr, zsend_r, zrecv_r, zsend_l, zrecv_l, y_own, y_recv, o_own, o_recv,
+    ga, wg, wgr, zsend, zrecv, y_own, y_recv, o_own, o_recv,
     send_sems, recv_sems,
 ):
     seq, head, z = lax.axis_index("seq"), lax.axis_index("head"), lax.axis_index("dp")
@@ -88,41 +88,73 @@
     xp, xm = dev(x_=at_x(1)), dev(x_=at_x(-1))
     yp, ym = dev(y_=at_y(1)), dev(y_=at_y(-1))
     zp, zm = dev(z_=at_z(1)), dev(z_=at_z(-1))
+    zp2, zm2 = dev(z_=at_z(2)), dev(z_=at_z(-2))
     mate = dev(c_=1 - c)
     pair = dev(y_=2 * yh + 1 - yl)
     cf, ylf = c.astype(F32), yl.astype(F32)
     go = Copies(send_sems, recv_sems)
 
     barrier = pltpu.get_barrier_semaphore()
-    for other in (xp, xm, yp, ym, zp, zm, mate):
+    for other in (xp, xm, yp, ym, zp, zm, zp2, zm2, mate):
         pl.semaphore_signal(barrier, inc=1, device_id=other, device_id_type=pl.DeviceIdType.MESH)
 
     def hs(i):
         return slice(i * DH, (i + 1) * DH)
 
+    quarter = 2 * c + yl
+    mine = c * 32
+    qown = pl.ds(pl.multiple_of(quarter * 256, 256), 256)
+    for a in range(3):
+        rows8 = (dp_ref[:, qown] if a == 0 else tab_ref[a - 1, :, qown]).astype(F32)
+        wz[3, a] = jnp.concatenate([rows8[:, :128], rows8[:, 128:]], axis=0).astype(BF16)
     for i in range(4):
         s_own[i] = dot_tn(k_ref[:, hs(i)], v_ref[:, hs(i)]).astype(BF16)
-    pl.semaphore_wait(barrier, 7)
-
-    quarter = 2 * c + yl
-    mine = c * 32
+    pl.semaphore_wait(barrier, 9)
 
     state_copy = go.send(s_own, s_recv, mate)
-    own_w = wp_ref.at[quarter]
     own_p = op_ref.at[pl.ds(pl.multiple_of(mine, 32), 32), :]
 
-    def w_slot(j):
-        return wz.at[j]
-
-    def p_slot(j):
-        return proj.at[j, c]
-
-    wr = go.send(own_w, w_slot(z), zp)
-    wl = go.send(own_w, w_slot(z), zm)
-    pr = go.send(own_p, p_slot(z), zp)
-    pll = go.send(own_p, p_slot(z), zm)
-    wz[z] = wp_ref[quarter]
+    w_came, p_came, to_mate = {}, {}, []
+
+    def slot(rel):
+        return (rel + 3) % nz
+
+    def send_wz(rel, hop, device):
+        w_came[rel - hop] = go.send(wz.at[slot(rel)], wz.at[slot(rel - hop)], device)
+
+    def send_p(rel, hop, device):
+        window = proj.at[at_z(rel), c]
+        p_came[rel - hop] = go.send(own_p if rel == 0 else window, window, device)
+
+    def p_wait(rel):
+        p_came[rel].wait_recv()
+        window = proj.at[at_z(rel), c]
+        to_mate.append(go.send(window, window, mate))
+
+    around = ((1, zp), (-1, zm), (2, zp2), (-2, zm2))
+    for hop, device in around:
+        send_wz(0, hop, device)
+    for hop, device in around:
+        send_p(0, hop, device)
     proj[z] = op_ref[...].reshape(2, 32, 512)
+
+    def relay_w(j):
+        for sign, device in ((-1, zp2), (1, zm2)):
+            for rel in (sign * (2 * j - 1), sign * 2 * j):
+                w_came[rel].wait_recv()
+                if rel != 6:
+                    send_wz(rel, -2 * sign, device)
+
+    def relay_p(j):
+        for sign, device in ((-1, zp2), (1, zm2)):
+            for rel in (sign * (2 * j - 1), sign * 2 * j):
+                p_came[rel].wait_recv()
+                if rel != 6:
+                    send_p(rel, -2 * sign, device)
+        for sign in (-1, 1):
+            for rel in (sign * (2 * j - 1), sign * 2 * j):
+                window = proj.at[at_z(rel), c]
+                to_mate.append(go.send(window, window, mate))
 
     rows = lax.broadcasted_iota(jnp.int32, (HALF, HALF), 0)
     cols = lax.broadcasted_iota(jnp.int32, (HALF, HALF), 1)
@@ -157,68 +189,98 @@
                 scale * (acc[:, hs(i)] + dot(q_ref[:, hs(i)], s_in[i]))
             ).astype(BF16)
 
-    pair_copy = None
-    to_mate = []
-    for step in range(1, 9):
-        wr.wait_recv()
-        if step < 8:
-            src = at_z(-step)
-            wr = go.send(w_slot(src), w_slot(src), zp)
-            wl.wait_recv()
-        if step < 7:
-            src = at_z(step)
-            wl = go.send(w_slot(src), w_slot(src), zm)
-        pr.wait_recv()
-        src = at_z(-step)
-        if step < 8:
-            pr = go.send(p_slot(src), p_slot(src), zp)
-        to_mate.append(go.send(p_slot(src), p_slot(src), mate))
-        if step < 8:
-            pll.wait_recv()
-            src = at_z(step)
-            if step < 7:
-                pll = go.send(p_slot(src), p_slot(src), zm)
-            to_mate.append(go.send(p_slot(src), p_slot(src), mate))
-        if step == 1:
-            pair_copy = pass_state()
-        if step <= 4:
-            forward(step - 1)
-        if step == 5:
-            finish_attended()
-
     q0 = pl.multiple_of(quarter * 256, 256)
-    c0 = pl.multiple_of(c * 512, 512)
-    for a in range(3):
-        for hf in range(2):
-            block = wz[hf * 8:hf * 8 + 8, a].astype(F32)
-            piece = jnp.concatenate(
-                [block[:, :8].reshape(64, 128), block[:, 8:].reshape(64, 128)], axis=1
-            )
-            wts[a, x, yh, hf, :, pl.ds(q0, 256)] = piece.astype(BF16)
+    ccols = pl.ds(pl.multiple_of(c * 512, 512), 512)
 
     def qcols(y_):
         return pl.ds(pl.multiple_of((2 * c + y_ % 2) * 256, 256), 256)
 
-    ccols = pl.ds(c0, 512)
-
-    def send_w(win, device):
+    def same(win, device):
         return go.send(win, win, device)
 
-    def wa_x(xx, r0=0, n=64):
-        return wts.at[:, xx, yh, 0, pl.ds(r0, n), qcols(y)]
-
-    def wb_y(yy, r0=0, n=64):
-        return wts.at[:, x, yy // 2, 1, pl.ds(r0, n), qcols(yy)]
-
-    def wa_y(a, yy, r0=0, n=64):
-        return wts.at[a, :, yy // 2, 0, pl.ds(r0, n), qcols(yy)]
-
-    def wb_x(a, xx, r0=0, n=64):
-        return wts.at[a, xx, :, 1, pl.ds(r0, n), ccols]
-
-    wax_p, wax_m = send_w(wa_x(x), xp), send_w(wa_x(x), xm)
-    wby_p, wby_m = send_w(wb_y(y), yp), send_w(wb_y(y), ym)
-
+    w_mate = []
+
+    class Plane:
+        def __init__(self, group):
+            self.g = group
+            for a in range(3):
+                block = wz[group * 8:group * 8 + 8, a].astype(F32)
+                piece = jnp.concatenate(
+                    [block[:, :8].reshape(64, 128), block[:, 8:].reshape(64, 128)], axis=1
+                )
+                wts[a, x, yh, group, :, pl.ds(q0, 256)] = piece.astype(BF16)
+            self.wait_for = (
+                same(self.ax(x, 0, 32), xp), same(self.ax(x, 0, 32), xm),
+                same(self.by(y, 32, 32), yp), same(self.by(y, 32, 32), ym),
+            )
+
+        def ax(self, xx, r0, n):
+            return wts.at[:, xx, yh, self.g, pl.ds(r0, n), qcols(y)]
+
+        def by(self, yy, r0, n):
+            return wts.at[:, x, yy // 2, self.g, pl.ds(r0, n), qcols(yy)]
+
+        def ay(self, yy, r0, n):
+            return wts.at[:, :, yy // 2, self.g, pl.ds(r0, n), qcols(yy)]
+
+        def bx(self, xx, r0, n):
+            return wts.at[:, xx, :, self.g, pl.ds(r0, n), ccols]
+
+        def arrived(self):
+            for copy in self.wait_for:
+                copy.wait_recv()
+
+        def second(self):
+            self.arrived()
+            self.wait_for = (
+                same(self.ax(at_x(-1), 0, 16), xp), same(self.ax(at_x(1), 16, 16), xm),
+                same(self.by(at_y(-1), 32, 16), yp), same(self.by(at_y(1), 48, 16), ym),
+            )
+
+        def third(self):
+            self.arrived()
+            self.wait_for = (
+                same(self.ay(y, 0, 32), yp), same(self.ay(y, 0, 32), ym),
+                same(self.bx(x, 32, 32), xp), same(self.bx(x, 32, 32), xm),
+            )
+            w_mate.append(same(self.ay(y, 0, 32), mate))
+            w_mate.append(same(self.bx(x, 32, 32), mate))
+
+        def fourth(self):
+            self.arrived()
+            self.wait_for = (
+                same(self.ay(at_y(-1), 0, 16), yp), same(self.ay(at_y(1), 16, 16), ym),
+                same(self.bx(at_x(-1), 32, 16), xp), same(self.bx(at_x(1), 48, 16), xm),
+            )
+            for step in (-1, 1):
+                w_mate.append(same(self.ay(at_y(step), 0, 32), mate))
+                w_mate.append(same(self.bx(at_x(step), 32, 32), mate))
+
+        def fifth(self):
+            self.arrived()
+            w_mate.append(same(self.ay(at_y(2), 0, 32), mate))
+            w_mate.append(same(self.bx(at_x(2), 32, 32), mate))
+
+    forward(0)
+    pair_copy = pass_state()
+    forward(1)
+    relay_w(1)
+    relay_p(1)
+    forward(2)
+    forward(3)
+    relay_w(2)
+    near = Plane(0)
+    relay_p(2)
+    finish_attended()
+    relay_w(3)
+    near.second()
+    relay_p(3)
+    for rel in (-7, -8, 7):
+        w_came[rel].wait_recv()
+    far = Plane(1)
+    near.third()
+    for rel in (-7, -8, 7):
+        p_wait(rel)
     for copy in to_mate:
         copy.wait_recv()
 
@@ -236,14 +298,7 @@
     max_p = go.send(mix.at[at_x(2), 0, :, :, pl.ds(0, 512)], ra1, xp)
     max_m = go.send(mix.at[at_x(2), 1, :, :, pl.ds(0, 512)], rb1, xm)
 
-    wax_p.wait_recv()
-    wax_m.wait_recv()
-    wax2_p = send_w(wa_x(at_x(-1), 0, 32), xp)
-    wax2_m = send_w(wa_x(at_x(1), 32, 32), xm)
-    wby_p.wait_recv()
-    wby_m.wait_recv()
-    wby2_p = send_w(wb_y(at_y(-1), 0, 32), yp)
-    wby2_m = send_w(wb_y(at_y(1), 32, 32), ym)
+    far.second()
 
     mby_p.wait_recv()
     mby_m.wait_recv()
@@ -260,44 +315,8 @@
     max2_p = go.send(mix.at[at_x(1), :, :, :, pl.ds(0, 512)], ra2, xp)
     max2_m = go.send(mix.at[at_x(-1), :, :, :, pl.ds(0, 512)], rb2, xm)
 
-    wax2_p.wait_recv()
-    wax2_m.wait_recv()
-    wby2_p.wait_recv()
-    wby2_m.wait_recv()
-    way, wbx = [None] * 3, [None] * 3
-    w_mate = []
-
-    def bulk(a):
-        way[a] = (send_w(wa_y(a, y), yp), send_w(wa_y(a, y), ym))
-        wbx[a] = (send_w(wb_x(a, x), xp), send_w(wb_x(a, x), xm))
-        w_mate.append(send_w(wa_y(a, y), mate))
-        w_mate.append(send_w(wb_x(a, x), mate))
-
-    way2, wbx2 = [None] * 3, [None] * 3
-
-    def bulk_relay(a):
-        for copy in way[a] + wbx[a]:
-            copy.wait_recv()
-        way2[a] = (
-            send_w(wa_y(a, at_y(-1), 0, 32), yp),
-            send_w(wa_y(a, at_y(1), 32, 32), ym),
-        )
-        wbx2[a] = (
-            send_w(wb_x(a, at_x(-1), 0, 32), xp),
-            send_w(wb_x(a, at_x(1), 32, 32), xm),
-        )
-        w_mate.append(send_w(wa_y(a, at_y(-1)), mate))
-        w_mate.append(send_w(wa_y(a, at_y(1)), mate))
-        w_mate.append(send_w(wb_x(a, at_x(-1)), mate))
-        w_mate.append(send_w(wb_x(a, at_x(1)), mate))
-
-    def bulk_end(a):
-        for copy in way2[a] + wbx2[a]:
-            copy.wait_recv()
-        w_mate.append(send_w(wa_y(a, at_y(2)), mate))
-        w_mate.append(send_w(wb_x(a, at_x(2)), mate))
-
-    bulk(1)
+    near.fourth()
+    far.third()
     mbf_p.wait_recv()
     mbf_m.wait_recv()
     for hf in range(2):
@@ -318,7 +337,7 @@
     mixed[:, al] = (
         mix[x, yh, :, :, al].astype(F32) + ra2[yh].astype(F32) + rb2[yh].astype(F32)
     ).reshape(64, 512)
-    bulk(0)
+    near.fifth()
     mbx_p.wait_recv()
     mbx_m.wait_recv()
     yb[at_x(1), 0] = (yb[at_x(1), 0].astype(F32) + sb1[0].astype(F32)).astype(BF16)
@@ -329,8 +348,7 @@
     may_m.wait_recv()
     maf_p = go.send(rar.at[0], raf.at[0], yp)
     maf_m = go.send(rar.at[1], raf.at[1], ym)
-    bulk(2)
-    bulk_relay(1)
+    far.fourth()
     maf_p.wait_recv()
     maf_m.wait_recv()
     mixed[:, al] = mixed[:, al] + raf[...].astype(F32).reshape(64, 512)
@@ -339,34 +357,39 @@
     mixed[:, be] = (
         yb[x].astype(F32) + sb2[0].astype(F32) + sb2[1].astype(F32)
     ).reshape(64, 512)
-    bulk_relay(0)
-    bulk_end(1)
-    bulk_relay(2)
-    bulk_end(0)
-    bulk_end(2)
+    far.fifth()
     for copy in w_mate:
         copy.wait_recv()
 
     def weight(a, xx):
         return wts[a, xx].reshape(256, 1024)
 
-    vocab = lax.broadcasted_iota(jnp.int32, (64, 1024), 1)
+    turn = (z * 8 + 128 - 24) % 128
+    place = lax.broadcasted_iota(jnp.int32, (256, 64), 0)
+    vocab = place - place % 128 + (place % 128 + turn) % 128
     for level in range(2):
-        onehot = jnp.where(ids_ref[:, level:level + 1] == vocab, 1.0, 0.0).astype(BF16)
+        ids = ids_ref[level:level + 1, :]
         total = None
         for xx in range(4):
-            term = dot(onehot[:, 256 * xx:256 * xx + 256], weight(1 + level, xx))
+            onehot = jnp.where(ids - 256 * xx == vocab, 1.0, 0.0).astype(BF16)
+            term = dot_tn(onehot, weight(1 + level, xx))
             total = term if total is None else total + term
         emb[level] = total
 
+    def turned(value, by):
+        return jnp.concatenate(
+            [pltpu.roll(value[:, 128 * j:128 * j + 128], by, 1) for j in range(8)], axis=1
+        )
+
     def back_through(g):
+        g = turned(g, (128 - turn) % 128).astype(BF16)
         total = None
         for xx in range(4):
             term = dot(g[:, 256 * xx:256 * xx + 256], weight(0, xx))
             total = term if total is None else total + term
         return total
 
-    gpre[...] = back_through(cot_ref[1])
+    gpre[...] = back_through(cot_ref[:, 1, :].astype(F32))
 
     def mean_of(value):
         return jnp.mean(value, axis=-1, keepdims=True)
@@ -375,23 +398,22 @@
     r1 = lax.rsqrt(mean_of(summed1 * summed1) + EPS)
     normed1 = (summed1 * r1).astype(BF16)
     mixed[...] = summed1
-    proj1 = jnp.concatenate([dot_nt(normed1, weight(0, xx)) for xx in range(4)], axis=1)
+    proj1 = turned(
+        jnp.concatenate([dot_nt(normed1, weight(0, xx)) for xx in range(4)], axis=1), turn
+    )
     sig = jax.nn.sigmoid(proj1)
     summed2 = summed1 + proj1 * sig + emb[1]
     r2 = lax.rsqrt(mean_of(summed2 * summed2) + EPS)
     g2 = gpre[...]
     gsum = r2 * g2 - summed2 * (r2 * r2 * r2 * mean_of(g2 * summed2))
     emb[0] = gsum
-    gproj = cot_ref[0].astype(F32) + gsum * (sig * (1.0 + proj1 * (1.0 - sig)))
-    g1 = back_through(gproj.astype(BF16))
+    gproj = cot_ref[:, 0, :].astype(F32) + gsum * (sig * (1.0 + proj1 * (1.0 - sig)))
+    g1 = back_through(gproj)
     summed1 = mixed[...]
     grad = emb[0] + r1 * g1 - summed1 * (r1 * r1 * r1 * mean_of(g1 * summed1))
     gb[x, yh] = grad.astype(BF16).reshape(2, 32, 1024)
 
     cal, cbe = pl.ds(0, 512), pl.ds(512, 512)
-
-    def same(win, device):
-        return go.send(win, win, device)
 
     def pieces(*idx):
         return gb.at[idx]
@@ -459,21 +481,22 @@
     def own_chunk(j):
         return wg[j, c].astype(F32) + wgr[j].astype(F32)
 
-    def ring_step(step, last_r, last_l):
-        if step <= 7:
-            value = own_chunk(at_z(8 - step))
-            if last_r is not None:
-                last_r.wait_recv()
-                value = value + zrecv_r[step - 2].astype(F32)
-            zsend_r[step - 1] = value.astype(BF16)
-            last_r = go.send(zsend_r.at[step - 1], zrecv_r.at[step - 1], zp)
-        value = own_chunk(at_z(step - 9))
-        if last_l is not None:
-            last_l.wait_recv()
-            value = value + zrecv_l[step - 2].astype(F32)
-        zsend_l[step - 1] = value.astype(BF16)
-        last_l = go.send(zsend_l.at[step - 1], zrecv_l.at[step - 1], zm)
-        return last_r, last_l
+    chains = ((8, 4), (7, 4), (-7, 4), (-6, 3))
+    came = [None] * 4
+
+    def chain_step(m):
+        for n, (first, length) in enumerate(chains):
+            if m >= length:
+                continue
+            sign = 1 if first > 0 else -1
+            dist = first - 2 * sign * m
+            value = own_chunk(at_z(dist))
+            if m > 0:
+                came[n].wait_recv()
+                value = value + zrecv[n, m - 1].astype(F32)
+            zsend[n, m] = value.astype(BF16)
+            device = {2: zp2, 1: zp, -1: zm, -2: zm2}[max(-2, min(2, dist))]
+            came[n] = go.send(zsend.at[n, m], zrecv.at[n, m], device)
 
     def backward(i):
         q0_, q1_ = q_ref[top, hs(i)], q_ref[bot, hs(i)]
@@ -495,24 +518,26 @@
         ).astype(BF16)
         gv_ref[bot, hs(i)] = (scale * (dot_tn(sc[i, 2], a1_) + dot(k1_, b))).astype(BF16)
 
-    last_r, last_l = ring_step(1, None, None)
+    chain_step(0)
     back_copy.wait_recv()
     bt_own[...] = (b_own[...].astype(F32) + b_recv[...].astype(F32)).astype(BF16)
     back_pair = go.send(bt_own, bt_recv, pair)
-    for step in range(2, 9):
-        last_r, last_l = ring_step(step, last_r if step <= 7 else last_r, last_l)
-        if step == 3:
-            back_pair.wait_recv()
-            b_in[...] = (
-                (1.0 - cf) * b_recv[...].astype(F32) + (1.0 - ylf) * bt_recv[...].astype(F32)
-            ).astype(BF16)
-        if 3 <= step <= 6:
-            backward(step - 3)
-    last_r.wait_recv()
-    last_l.wait_recv()
-    y_own[...] = (
-        own_chunk(z) + zrecv_r[6].astype(F32) + zrecv_l[7].astype(F32)
+    chain_step(1)
+    back_pair.wait_recv()
+    b_in[...] = (
+        (1.0 - cf) * b_recv[...].astype(F32) + (1.0 - ylf) * bt_recv[...].astype(F32)
     ).astype(BF16)
+    backward(0)
+    backward(1)
+    chain_step(2)
+    backward(2)
+    chain_step(3)
+    backward(3)
+    total = own_chunk(z)
+    for n, (first, length) in enumerate(chains):
+        came[n].wait_recv()
+        total = total + zrecv[n, length - 1].astype(F32)
+    y_own[...] = total.astype(BF16)
     y_copy = go.send(y_own, y_recv, pair)
     y_copy.wait_recv()
     o_own[...] = y_own[...].astype(F32) + y_recv[...].astype(F32)
@@ -525,12 +550,6 @@
 
 def on_device(queries, keys, values, out_proj, depth_proj, code_table, code_ids, depth_cotangent):
     scale = 2048.0 ** (-0.5)
-    stacked = jnp.concatenate([depth_proj.T[None], code_table], axis=0)
-    packed = (
-        stacked.reshape(3, 8, 4, 2, 128).transpose(2, 0, 3, 1, 4).reshape(4, 3, 16, 128)
-    )
-    cot = jnp.transpose(depth_cotangent[0], (1, 0, 2))
-
     def vm(shape, kind=BF16):
         return pltpu.VMEM(shape, kind)
 
@@ -543,7 +562,7 @@
             jax.ShapeDtypeStruct((512, 512), BF16),
             jax.ShapeDtypeStruct((64, 512), F32),
         ),
-        in_specs=[pl.BlockSpec(memory_space=pltpu.VMEM)] * 7,
+        in_specs=[pl.BlockSpec(memory_space=pltpu.VMEM)] * 8,
         out_specs=(pl.BlockSpec(memory_space=pltpu.VMEM),) * 4,
         scratch_shapes=[
             vm((16, 3, 16, 128)), vm((16, 2, 32, 512)), vm((3, 4, 2, 2, 64, 1024)),
@@ -559,17 +578,18 @@
             vm((64, 1024), F32), vm((2, 64, 1024), F32), vm((64, 1024), F32),
             vm((4, 2, 2, 32, 1024)), vm((2, 4, 32, 512)), vm((2, 32, 512)),
             vm((512, 512)), vm((16, 2, 32, 512)), vm((16, 32, 512)),
-            vm((7, 32, 512)), vm((7, 32, 512)), vm((8, 32, 512)), vm((8, 32, 512)),
+            vm((4, 4, 32, 512)), vm((4, 4, 32, 512)),
             vm((32, 512)), vm((32, 512)), vm((32, 512), F32), vm((32, 512), F32),
             pltpu.SemaphoreType.DMA((N_COPIES,)),
             pltpu.SemaphoreType.DMA((N_COPIES,)),
         ],
         compiler_params=pltpu.CompilerParams(
-            collective_id=0, has_side_effects=True, vmem_limit_bytes=60 * 1024 * 1024
+            collective_id=0, has_side_effects=True, vmem_limit_bytes=34 * 1024 * 1024
         ),
         name="fused_step",
     )(
-        queries[0], keys[0], values[0], out_proj.T, packed, code_ids[0], cot,
+        queries[0], keys[0], values[0], out_proj.T, depth_proj.T, code_table, code_ids[0].T,
+        depth_cotangent[0],
     )
     return gq[None], gk[None], gv[None], gop.T
 

time: 135 us -> 119 us (0.88)
  Pallas kernels: 125 us -> 108 us
  local copies, waits for them, and re-layouts: 7.93 us -> 10.1 us
    pallas_call x1, Pallas kernels: 125 us -> 108 us  [on_device(): pl.pallas_call(functools.partial(kernel, scale), out_shape=(jax.ShapeDtyp...]
    unnamed x13 -> x20, local copies, waits for them, and re-layouts: 6.54 us -> 10.1 us
    squeeze x1 -> x0, local copies, waits for them, and re-layouts: 1.39 us -> none  [on_device(): code_ids[0]]
where the time goes in v2:
time: 119 us
  Pallas kernels  108 us (91%)
  local copies, waits for them, and re-layouts  10.1 us (8%)
    pallas_call x1, Pallas kernels, on_device(): pl.pallas_call(functools.partial(kernel, scale), out_shape=(jax.ShapeDtyp...  108 us
    unnamed x20, local copies, waits for them, and re-layouts  10.1 us

profile of v2, /device:TPU:1, one launch (start us, length us, event | category | flops | bytes accessed | tf_op | source)
XLA Modules:
  0.0 118.9 jit_solution(14314800789525798841)
XLA Ops:
  0.6 0.0 copy-start.7
  0.6 0.7 copy-done.7
  1.3 0.0 copy-start
  1.3 1.0 copy-done
  2.4 0.0 copy-start.1
  2.4 1.0 copy-done.1
  3.4 0.0 copy-start.2
  3.4 1.0 copy-done.2
  4.4 0.0 copy-start.3
  4.4 0.9 copy-done.3
  5.4 0.0 copy-start.4
  5.4 0.8 copy-done.4
  6.2 0.0 copy-start.5
  6.2 0.8 copy-done.5
  7.0 0.0 copy-start.6
  7.0 0.7 copy-done.6
  7.7 108.1 %fused_step.1 = (bf16[512,512]{1,0:T(8,128)(2,1)S(1)}, bf16[512,512]{1,0:T(8,128)(2,1)S(1)}, bf16[512,512]{1,0:T(8,128)(2,1)S(1)}, f32[64,512]{1,0:T(8,128)S(1)}) custom-call(bf16[512,512]{1,0:T(8,128)(2,1)S(1)} %bitcast.13, bf16[512,512]{1,0:T(8,128)(2,1)S(1)} %bitcast.14, bf16[512,512]{1,0:T(8,128)(2,1)S(1)} %bitcast.15, bf16[64,512]{1,0:T(8,128)(2,1)S(1)} %bitcast.21, ...), custom_call_target="tpu_custom_call" | custom-call | tf_op jit(solution)/shard_map/fused_step/pallas_call | solution.py:557
  115.8 0.8 copy.16
  116.6 0.8 copy.17
  117.4 0.8 copy.18
  118.2 0.7 copy.19
Async XLA Ops:
  0.6 0.7 copy-start.7
  1.3 1.0 copy-start
  2.4 1.0 copy-start.1
  3.4 1.0 copy-start.2
  4.4 0.9 copy-start.3
  5.4 0.8 copy-start.4
  6.2 0.8 copy-start.5
  7.0 0.7 copy-start.6

commit v3 on v2

--- a/solution.py
+++ b/solution.py
@@ -52,8 +52,9 @@
 
 def kernel(
     scale,
-    q_ref, k_ref, v_ref, op_ref, dp_ref, tab_ref, ids_ref, cot_ref,
+    q_in, k_in, v_in, op_in, dp_in, tab_in, ids_in, cot_in,
     gq_ref, gk_ref, gv_ref, go_ref,
+    q_ref, k_ref, v_ref, op_ref, dp_ref, tab_ref, ids_ref, cot_ref, load_sems,
     wz, proj, wts,
     s_own, s_recv, t_own, t_recv, s_in,
     b_own, b_recv, bt_own, bt_recv, b_in,
@@ -101,20 +102,35 @@
     def hs(i):
         return slice(i * DH, (i + 1) * DH)
 
+    loads = [
+        pltpu.make_async_copy(src, dst, load_sems.at[n])
+        for n, (src, dst) in enumerate((
+            (dp_in, dp_ref), (tab_in, tab_ref), (k_in, k_ref), (v_in, v_ref),
+            (q_in, q_ref), (op_in, op_ref), (ids_in, ids_ref), (cot_in, cot_ref),
+        ))
+    ]
+    for load in loads:
+        load.start()
     quarter = 2 * c + yl
+    loads[0].wait()
+    loads[1].wait()
     mine = c * 32
     qown = pl.ds(pl.multiple_of(quarter * 256, 256), 256)
     for a in range(3):
         rows8 = (dp_ref[:, qown] if a == 0 else tab_ref[a - 1, :, qown]).astype(F32)
         wz[3, a] = jnp.concatenate([rows8[:, :128], rows8[:, 128:]], axis=0).astype(BF16)
+    loads[2].wait()
+    loads[3].wait()
     for i in range(4):
         s_own[i] = dot_tn(k_ref[:, hs(i)], v_ref[:, hs(i)]).astype(BF16)
+    for load in loads[4:]:
+        load.wait()
     pl.semaphore_wait(barrier, 9)
 
     state_copy = go.send(s_own, s_recv, mate)
     own_p = op_ref.at[pl.ds(pl.multiple_of(mine, 32), 32), :]
 
-    w_came, p_came, to_mate = {}, {}, []
+    w_came, p_came, to_mate = {}, {}, {}
 
     def slot(rel):
         return (rel + 3) % nz
@@ -123,20 +139,19 @@
         w_came[rel - hop] = go.send(wz.at[slot(rel)], wz.at[slot(rel - hop)], device)
 
     def send_p(rel, hop, device):
-        window = proj.at[at_z(rel), c]
-        p_came[rel - hop] = go.send(own_p if rel == 0 else window, window, device)
-
-    def p_wait(rel):
-        p_came[rel].wait_recv()
-        window = proj.at[at_z(rel), c]
-        to_mate.append(go.send(window, window, mate))
+        src = own_p if rel == 0 else proj.at[slot(rel), c]
+        p_came[rel - hop] = go.send(src, proj.at[slot(rel - hop), c], device)
+
+    def p_mate(rel):
+        window = proj.at[slot(rel), c]
+        to_mate[rel] = go.send(window, window, mate)
 
     around = ((1, zp), (-1, zm), (2, zp2), (-2, zm2))
     for hop, device in around:
         send_wz(0, hop, device)
     for hop, device in around:
         send_p(0, hop, device)
-    proj[z] = op_ref[...].reshape(2, 32, 512)
+    proj[3] = op_ref[...].reshape(2, 32, 512)
 
     def relay_w(j):
         for sign, device in ((-1, zp2), (1, zm2)):
@@ -153,8 +168,7 @@
                     send_p(rel, -2 * sign, device)
         for sign in (-1, 1):
             for rel in (sign * (2 * j - 1), sign * 2 * j):
-                window = proj.at[at_z(rel), c]
-                to_mate.append(go.send(window, window, mate))
+                p_mate(rel)
 
     rows = lax.broadcasted_iota(jnp.int32, (HALF, HALF), 0)
     cols = lax.broadcasted_iota(jnp.int32, (HALF, HALF), 1)
@@ -261,6 +275,102 @@
             w_mate.append(same(self.ay(at_y(2), 0, 32), mate))
             w_mate.append(same(self.bx(at_x(2), 32, 32), mate))
 
+    class Reduce:
+        def __init__(self, group):
+            self.g, self.a0, self.b0 = group, 512 * group, 512 * group + 256
+            self.block(2 * group + 1)
+            b = pl.ds(self.b0, 256)
+            self.y1 = (
+                go.send(mix.at[:, 1 - yh, 0, :, b], rbr.at[group, 0], yp),
+                go.send(mix.at[:, 1 - yh, 1, :, b], rbr.at[group, 1], ym),
+            )
+            self.block(2 * group)
+            a = pl.ds(self.a0, 256)
+            self.x1 = (
+                go.send(mix.at[at_x(2), 0, :, :, a], ra1.at[group], xp),
+                go.send(mix.at[at_x(2), 1, :, :, a], rb1.at[group], xm),
+            )
+
+        def block(self, j):
+            part = dot_nt(att[...], proj[4 * j:4 * j + 4].reshape(256, 512))
+            mix[:, :, :, :, 256 * j:256 * j + 256] = part.astype(BF16).reshape(4, 2, 2, 32, 256)
+
+        def second(self):
+            g, al = self.g, slice(self.a0, self.a0 + 256)
+            for copy in self.y1:
+                copy.wait_recv()
+            self.y2 = (
+                go.send(rbr.at[g, 0], rbf.at[g, 0], yp), go.send(rbr.at[g, 1], rbf.at[g, 1], ym)
+            )
+            for copy in self.x1:
+                copy.wait_recv()
+            mix[at_x(1), 0, :, :, al] = (
+                mix[at_x(1), 0, :, :, al].astype(F32) + ra1[g].astype(F32)
+            ).astype(BF16)
+            mix[at_x(-1), 1, :, :, al] = (
+                mix[at_x(-1), 1, :, :, al].astype(F32) + rb1[g].astype(F32)
+            ).astype(BF16)
+            a = pl.ds(self.a0, 256)
+            self.x2 = (
+                go.send(mix.at[at_x(1), :, :, :, a], ra2.at[g], xp),
+                go.send(mix.at[at_x(-1), :, :, :, a], rb2.at[g], xm),
+            )
+
+        def third(self):
+            g, al, be = self.g, slice(self.a0, self.a0 + 256), slice(self.b0, self.b0 + 256)
+            for copy in self.y2:
+                copy.wait_recv()
+            for hf in range(2):
+                yb[g, :, hf] = (
+                    mix[:, yh, hf, :, be].astype(F32) + rbf[g, hf].astype(F32)
+                ).astype(BF16)
+            self.bx1 = (
+                go.send(yb.at[g, at_x(2), 0], sb1.at[g, 0], xp),
+                go.send(yb.at[g, at_x(2), 1], sb1.at[g, 1], xm),
+            )
+            for copy in self.x2:
+                copy.wait_recv()
+            ray[g] = (
+                mix[x, 1 - yh, :, :, al].astype(F32)
+                + ra2[g, 1 - yh].astype(F32)
+                + rb2[g, 1 - yh].astype(F32)
+            ).astype(BF16)
+            self.ay1 = (
+                go.send(ray.at[g, 0], rar.at[g, 0], yp), go.send(ray.at[g, 1], rar.at[g, 1], ym)
+            )
+            mixed[:, al] = (
+                mix[x, yh, :, :, al].astype(F32)
+                + ra2[g, yh].astype(F32)
+                + rb2[g, yh].astype(F32)
+            ).reshape(64, 256)
+
+        def fourth(self):
+            g = self.g
+            for copy in self.bx1:
+                copy.wait_recv()
+            for step, hf in ((1, 0), (-1, 1)):
+                yb[g, at_x(step), hf] = (
+                    yb[g, at_x(step), hf].astype(F32) + sb1[g, hf].astype(F32)
+                ).astype(BF16)
+            self.bx2 = (
+                go.send(yb.at[g, at_x(1)], sb2.at[g, 0], xp),
+                go.send(yb.at[g, at_x(-1)], sb2.at[g, 1], xm),
+            )
+            for copy in self.ay1:
+                copy.wait_recv()
+            self.ay2 = (
+                go.send(rar.at[g, 0], raf.at[g, 0], yp), go.send(rar.at[g, 1], raf.at[g, 1], ym)
+            )
+
+        def fifth(self):
+            g, al, be = self.g, slice(self.a0, self.a0 + 256), slice(self.b0, self.b0 + 256)
+            for copy in self.ay2 + self.bx2:
+                copy.wait_recv()
+            mixed[:, al] = mixed[:, al] + raf[g].astype(F32).reshape(64, 256)
+            mixed[:, be] = (
+                yb[g, x].astype(F32) + sb2[g, 0].astype(F32) + sb2[g, 1].astype(F32)
+            ).reshape(64, 256)
+
     forward(0)
     pair_copy = pass_state()
     forward(1)
@@ -272,91 +382,35 @@
     near = Plane(0)
     relay_p(2)
     finish_attended()
+    near.second()
+    for rel in (-1, -2, 1, 2, -3, 3, 4):
+        to_mate[rel].wait_recv()
+    mnear = Reduce(0)
     relay_w(3)
-    near.second()
+    near.third()
     relay_p(3)
+    mnear.second()
     for rel in (-7, -8, 7):
         w_came[rel].wait_recv()
     far = Plane(1)
-    near.third()
+    mnear.third()
     for rel in (-7, -8, 7):
-        p_wait(rel)
-    for copy in to_mate:
-        copy.wait_recv()
-
-    def mix_block(j):
-        part = dot_nt(att[...], proj[4 * j:4 * j + 4].reshape(256, 512))
-        mix[:, :, :, :, 256 * j:256 * j + 256] = part.astype(BF16).reshape(4, 2, 2, 32, 256)
-
-    al, be = slice(0, 512), slice(512, 1024)
-    mix_block(2)
-    mix_block(3)
-    mby_p = go.send(mix.at[:, 1 - yh, 0, :, pl.ds(512, 512)], rbr.at[0], yp)
-    mby_m = go.send(mix.at[:, 1 - yh, 1, :, pl.ds(512, 512)], rbr.at[1], ym)
-    mix_block(0)
-    mix_block(1)
-    max_p = go.send(mix.at[at_x(2), 0, :, :, pl.ds(0, 512)], ra1, xp)
-    max_m = go.send(mix.at[at_x(2), 1, :, :, pl.ds(0, 512)], rb1, xm)
-
+        p_came[rel].wait_recv()
+        p_mate(rel)
+    for rel in (-4, -5, -6, 5, 6, -7, -8, 7):
+        to_mate[rel].wait_recv()
+    mfar = Reduce(1)
     far.second()
-
-    mby_p.wait_recv()
-    mby_m.wait_recv()
-    mbf_p = go.send(rbr.at[0], rbf.at[0], yp)
-    mbf_m = go.send(rbr.at[1], rbf.at[1], ym)
-    max_p.wait_recv()
-    max_m.wait_recv()
-    mix[at_x(1), 0, :, :, al] = (
-        mix[at_x(1), 0, :, :, al].astype(F32) + ra1[...].astype(F32)
-    ).astype(BF16)
-    mix[at_x(-1), 1, :, :, al] = (
-        mix[at_x(-1), 1, :, :, al].astype(F32) + rb1[...].astype(F32)
-    ).astype(BF16)
-    max2_p = go.send(mix.at[at_x(1), :, :, :, pl.ds(0, 512)], ra2, xp)
-    max2_m = go.send(mix.at[at_x(-1), :, :, :, pl.ds(0, 512)], rb2, xm)
-
+    mnear.fourth()
     near.fourth()
+    mfar.second()
     far.third()
-    mbf_p.wait_recv()
-    mbf_m.wait_recv()
-    for hf in range(2):
-        yb[:, hf] = (
-            mix[:, yh, hf, :, be].astype(F32) + rbf[hf].astype(F32)
-        ).astype(BF16)
-    mbx_p = go.send(yb.at[at_x(2), 0], sb1.at[0], xp)
-    mbx_m = go.send(yb.at[at_x(2), 1], sb1.at[1], xm)
-    max2_p.wait_recv()
-    max2_m.wait_recv()
-    ray[...] = (
-        mix[x, 1 - yh, :, :, al].astype(F32)
-        + ra2[1 - yh].astype(F32)
-        + rb2[1 - yh].astype(F32)
-    ).astype(BF16)
-    may_p = go.send(ray.at[0], rar.at[0], yp)
-    may_m = go.send(ray.at[1], rar.at[1], ym)
-    mixed[:, al] = (
-        mix[x, yh, :, :, al].astype(F32) + ra2[yh].astype(F32) + rb2[yh].astype(F32)
-    ).reshape(64, 512)
+    mnear.fifth()
+    mfar.third()
     near.fifth()
-    mbx_p.wait_recv()
-    mbx_m.wait_recv()
-    yb[at_x(1), 0] = (yb[at_x(1), 0].astype(F32) + sb1[0].astype(F32)).astype(BF16)
-    yb[at_x(-1), 1] = (yb[at_x(-1), 1].astype(F32) + sb1[1].astype(F32)).astype(BF16)
-    mbx2_p = go.send(yb.at[at_x(1)], sb2.at[0], xp)
-    mbx2_m = go.send(yb.at[at_x(-1)], sb2.at[1], xm)
-    may_p.wait_recv()
-    may_m.wait_recv()
-    maf_p = go.send(rar.at[0], raf.at[0], yp)
-    maf_m = go.send(rar.at[1], raf.at[1], ym)
+    mfar.fourth()
     far.fourth()
-    maf_p.wait_recv()
-    maf_m.wait_recv()
-    mixed[:, al] = mixed[:, al] + raf[...].astype(F32).reshape(64, 512)
-    mbx2_p.wait_recv()
-    mbx2_m.wait_recv()
-    mixed[:, be] = (
-        yb[x].astype(F32) + sb2[0].astype(F32) + sb2[1].astype(F32)
-    ).reshape(64, 512)
+    mfar.fifth()
     far.fifth()
     for copy in w_mate:
         copy.wait_recv()
@@ -394,7 +448,8 @@
     def mean_of(value):
         return jnp.mean(value, axis=-1, keepdims=True)
 
-    summed1 = mixed[...] + emb[0]
+    shift = (z * 64 + 1024 - 192) % 1024
+    summed1 = pltpu.roll(mixed[...], shift, 1) + emb[0]
     r1 = lax.rsqrt(mean_of(summed1 * summed1) + EPS)
     normed1 = (summed1 * r1).astype(BF16)
     mixed[...] = summed1
@@ -411,56 +466,107 @@
     g1 = back_through(gproj)
     summed1 = mixed[...]
     grad = emb[0] + r1 * g1 - summed1 * (r1 * r1 * r1 * mean_of(g1 * summed1))
+    grad = pltpu.roll(grad, (1024 - shift) % 1024, 1)
     gb[x, yh] = grad.astype(BF16).reshape(2, 32, 1024)
 
-    cal, cbe = pl.ds(0, 512), pl.ds(512, 512)
-
-    def pieces(*idx):
-        return gb.at[idx]
-
-    bx1_p = go.send(pieces(x, yh, 0, slice(None), cbe), grb.at[0], yp)
-    bx1_m = go.send(pieces(x, yh, 1, slice(None), cbe), grb.at[1], ym)
-    own_a = gb.at[x, yh, :, :, cal]
-    ax_p, ax_m = same(own_a, xp), same(own_a, xm)
-    bx1_p.wait_recv()
-    bx1_m.wait_recv()
-    b2_p = go.send(grb.at[0], gb.at[x, at_y(-1) // 2, 0, :, cbe], yp)
-    b2_m = go.send(grb.at[1], gb.at[x, at_y(1) // 2, 1, :, cbe], ym)
-    ax_p.wait_recv()
-    ax_m.wait_recv()
-    ax2_p = same(gb.at[at_x(-1), yh, 0, :, cal], xp)
-    ax2_m = same(gb.at[at_x(1), yh, 1, :, cal], xm)
-    b2_p.wait_recv()
-    b2_m.wait_recv()
-    own_b = gb.at[x, :, :, :, cbe]
-    bx_p, bx_m = same(own_b, xp), same(own_b, xm)
-    ax2_p.wait_recv()
-    ax2_m.wait_recv()
-    ay_p = go.send(gb.at[:, yh, 0, :, cal], gra.at[0], yp)
-    ay_m = go.send(gb.at[:, yh, 1, :, cal], gra.at[1], ym)
-    bx_p.wait_recv()
-    bx_m.wait_recv()
-    bx2_p = same(gb.at[at_x(-1), 0, :, :, cbe], xp)
-    bx2_m = same(gb.at[at_x(1), 1, :, :, cbe], xm)
-    ay_p.wait_recv()
-    ay_m.wait_recv()
-    af_p = go.send(gra.at[0], gb.at[:, at_y(-1) // 2, 0, :, cal], yp)
-    af_m = go.send(gra.at[1], gb.at[:, at_y(1) // 2, 1, :, cal], ym)
+    class Spread:
+        def __init__(self, group):
+            self.g, self.a, self.b = group, pl.ds(512 * group, 256), pl.ds(512 * group + 256, 256)
+            self.y1 = (
+                go.send(gb.at[x, yh, 0, :, self.b], grb.at[group, 0], yp),
+                go.send(gb.at[x, yh, 1, :, self.b], grb.at[group, 1], ym),
+            )
+            own = gb.at[x, yh, :, :, self.a]
+            self.x1 = (same(own, xp), same(own, xm))
+
+        def second(self):
+            for copy in self.y1:
+                copy.wait_recv()
+            self.y2 = (
+                go.send(grb.at[self.g, 0], gb.at[x, at_y(-1) // 2, 0, :, self.b], yp),
+                go.send(grb.at[self.g, 1], gb.at[x, at_y(1) // 2, 1, :, self.b], ym),
+            )
+            for copy in self.x1:
+                copy.wait_recv()
+            self.x2 = (
+                same(gb.at[at_x(-1), yh, 0, :, self.a], xp),
+                same(gb.at[at_x(1), yh, 1, :, self.a], xm),
+            )
+
+        def third(self):
+            for copy in self.y2:
+                copy.wait_recv()
+            own = gb.at[x, :, :, :, self.b]
+            self.bx1 = (same(own, xp), same(own, xm))
+            for copy in self.x2:
+                copy.wait_recv()
+            self.ay1 = (
+                go.send(gb.at[:, yh, 0, :, self.a], gra.at[self.g, 0], yp),
+                go.send(gb.at[:, yh, 1, :, self.a], gra.at[self.g, 1], ym),
+            )
+
+        def fourth(self):
+            for copy in self.bx1:
+                copy.wait_recv()
+            self.bx2 = (
+                same(gb.at[at_x(-1), 0, :, :, self.b], xp),
+                same(gb.at[at_x(1), 1, :, :, self.b], xm),
+            )
+            for copy in self.ay1:
+                copy.wait_recv()
+            self.ay2 = (
+                go.send(gra.at[self.g, 0], gb.at[:, at_y(-1) // 2, 0, :, self.a], yp),
+                go.send(gra.at[self.g, 1], gb.at[:, at_y(1) // 2, 1, :, self.a], ym),
+            )
+
+        def fifth(self):
+            for copy in self.bx2 + self.ay2:
+                copy.wait_recv()
 
     def weight_grad(j):
         block = gb[:, :, :, :, 256 * j:256 * j + 256].reshape(512, 256)
         wg[4 * j:4 * j + 4] = dot_tn(block, att[...]).astype(BF16).reshape(4, 2, 32, 512)
 
-    bx2_p.wait_recv()
-    bx2_m.wait_recv()
-    weight_grad(2)
-    weight_grad(3)
-    wg_b = go.send(wg.at[pl.ds(8, 8), 1 - c], wgr.at[pl.ds(8, 8)], mate)
-    af_p.wait_recv()
-    af_m.wait_recv()
-    weight_grad(0)
-    weight_grad(1)
-    wg_a = go.send(wg.at[pl.ds(0, 8), 1 - c], wgr.at[pl.ds(0, 8)], mate)
+    def halves(group):
+        weight_grad(2 * group)
+        weight_grad(2 * group + 1)
+        rows8 = pl.ds(8 * group, 8)
+        return go.send(wg.at[rows8, 1 - c], wgr.at[rows8], mate)
+
+    def own_chunk(rel):
+        return wg[slot(rel), c].astype(F32) + wgr[slot(rel)].astype(F32)
+
+    chains = ((8, 4), (7, 4), (-7, 4), (-6, 3))
+    came = [None] * 4
+
+    def chain_step(m):
+        for n, (first, length) in enumerate(chains):
+            if m >= length:
+                continue
+            sign = 1 if first > 0 else -1
+            dist = first - 2 * sign * m
+            value = own_chunk(dist)
+            if m > 0:
+                came[n].wait_recv()
+                value = value + zrecv[n, m - 1].astype(F32)
+            zsend[n, m] = value.astype(BF16)
+            device = {2: zp2, 1: zp, -1: zm, -2: zm2}[max(-2, min(2, dist))]
+            came[n] = go.send(zsend.at[n, m], zrecv.at[n, m], device)
+
+    spread_far = Spread(1)
+    spread_near = Spread(0)
+    spread_far.second()
+    spread_near.second()
+    spread_far.third()
+    spread_near.third()
+    spread_far.fourth()
+    spread_far.fifth()
+    wg_far = halves(1)
+    spread_near.fourth()
+    wg_far.wait_recv()
+    chain_step(0)
+    spread_near.fifth()
+    wg_near = halves(0)
 
     for j in range(2):
         total = None
@@ -475,28 +581,6 @@
     for i in range(4):
         b_own[i] = dot_tn(q_ref[:, hs(i)], ga[:, hs(i)]).astype(BF16)
     back_copy = go.send(b_own, b_recv, mate)
-    wg_b.wait_recv()
-    wg_a.wait_recv()
-
-    def own_chunk(j):
-        return wg[j, c].astype(F32) + wgr[j].astype(F32)
-
-    chains = ((8, 4), (7, 4), (-7, 4), (-6, 3))
-    came = [None] * 4
-
-    def chain_step(m):
-        for n, (first, length) in enumerate(chains):
-            if m >= length:
-                continue
-            sign = 1 if first > 0 else -1
-            dist = first - 2 * sign * m
-            value = own_chunk(at_z(dist))
-            if m > 0:
-                came[n].wait_recv()
-                value = value + zrecv[n, m - 1].astype(F32)
-            zsend[n, m] = value.astype(BF16)
-            device = {2: zp2, 1: zp, -1: zm, -2: zm2}[max(-2, min(2, dist))]
-            came[n] = go.send(zsend.at[n, m], zrecv.at[n, m], device)
 
     def backward(i):
         q0_, q1_ = q_ref[top, hs(i)], q_ref[bot, hs(i)]
@@ -518,22 +602,22 @@
         ).astype(BF16)
         gv_ref[bot, hs(i)] = (scale * (dot_tn(sc[i, 2], a1_) + dot(k1_, b))).astype(BF16)
 
-    chain_step(0)
+    chain_step(1)
     back_copy.wait_recv()
     bt_own[...] = (b_own[...].astype(F32) + b_recv[...].astype(F32)).astype(BF16)
     back_pair = go.send(bt_own, bt_recv, pair)
-    chain_step(1)
+    wg_near.wait_recv()
     back_pair.wait_recv()
     b_in[...] = (
         (1.0 - cf) * b_recv[...].astype(F32) + (1.0 - ylf) * bt_recv[...].astype(F32)
     ).astype(BF16)
     backward(0)
+    chain_step(2)
     backward(1)
-    chain_step(2)
     backward(2)
     chain_step(3)
     backward(3)
-    total = own_chunk(z)
+    total = own_chunk(0)
     for n, (first, length) in enumerate(chains):
         came[n].wait_recv()
         total = total + zrecv[n, length - 1].astype(F32)
@@ -548,6 +632,28 @@
     go.drain()
 
 
+def out_kernel(*refs):
+    copies = [
+        pltpu.make_async_copy(refs[n], refs[4 + n], refs[8].at[n]) for n in range(4)
+    ]
+    for copy in copies:
+        copy.start()
+    for copy in copies:
+        copy.wait()
+
+
+def write_out(*arrays):
+    return pl.pallas_call(
+        out_kernel,
+        out_shape=tuple(jax.ShapeDtypeStruct(a.shape, a.dtype) for a in arrays),
+        in_specs=[pl.BlockSpec(memory_space=pltpu.VMEM)] * 4,
+        out_specs=(pl.BlockSpec(memory_space=pltpu.HBM),) * 4,
+        scratch_shapes=[pltpu.SemaphoreType.DMA((4,))],
+        compiler_params=pltpu.CompilerParams(vmem_limit_bytes=8 * 1024 * 1024),
+        name="write_out",
+    )(*arrays)
+
+
 def on_device(queries, keys, values, out_proj, depth_proj, code_table, code_ids, depth_cotangent):
     scale = 2048.0 ** (-0.5)
     def vm(shape, kind=BF16):
@@ -562,21 +668,24 @@
             jax.ShapeDtypeStruct((512, 512), BF16),
             jax.ShapeDtypeStruct((64, 512), F32),
         ),
-        in_specs=[pl.BlockSpec(memory_space=pltpu.VMEM)] * 8,
+        in_specs=[pl.BlockSpec(memory_space=pltpu.HBM)] * 8,
         out_specs=(pl.BlockSpec(memory_space=pltpu.VMEM),) * 4,
         scratch_shapes=[
+            vm((512, 512)), vm((512, 512)), vm((512, 512)), vm((64, 512)),
+            vm((8, 1024)), vm((2, 8, 1024)), vm((2, 64), jnp.int32), vm((64, 2, 1024)),
+            pltpu.SemaphoreType.DMA((8,)),
             vm((16, 3, 16, 128)), vm((16, 2, 32, 512)), vm((3, 4, 2, 2, 64, 1024)),
             state, state, state, state, state,
             state, state, state, state, state,
             vm((4, 3, 256, 256)), vm((512, 512), F32), vm((512, 512)),
             vm((4, 2, 2, 32, 1024)),
-            vm((2, 32, 512)), vm((2, 32, 512)),
-            vm((2, 2, 32, 512)), vm((2, 2, 32, 512)),
-            vm((2, 32, 512)), vm((2, 32, 512)), vm((2, 32, 512)),
-            vm((2, 4, 32, 512)), vm((2, 4, 32, 512)),
-            vm((4, 2, 32, 512)), vm((2, 32, 512)), vm((2, 2, 32, 512)),
+            vm((2, 2, 32, 256)), vm((2, 2, 32, 256)),
+            vm((2, 2, 2, 32, 256)), vm((2, 2, 2, 32, 256)),
+            vm((2, 2, 32, 256)), vm((2, 2, 32, 256)), vm((2, 2, 32, 256)),
+            vm((2, 2, 4, 32, 256)), vm((2, 2, 4, 32, 256)),
+            vm((2, 4, 2, 32, 256)), vm((2, 2, 32, 256)), vm((2, 2, 2, 32, 256)),
             vm((64, 1024), F32), vm((2, 64, 1024), F32), vm((64, 1024), F32),
-            vm((4, 2, 2, 32, 1024)), vm((2, 4, 32, 512)), vm((2, 32, 512)),
+            vm((4, 2, 2, 32, 1024)), vm((2, 2, 4, 32, 256)), vm((2, 2, 32, 256)),
             vm((512, 512)), vm((16, 2, 32, 512)), vm((16, 32, 512)),
             vm((4, 4, 32, 512)), vm((4, 4, 32, 512)),
             vm((32, 512)), vm((32, 512)), vm((32, 512), F32), vm((32, 512), F32),
@@ -588,9 +697,15 @@
         ),
         name="fused_step",
     )(
-        queries[0], keys[0], values[0], out_proj.T, depth_proj.T, code_table, code_ids[0].T,
-        depth_cotangent[0],
+        *(
+            pltpu.with_memory_space_constraint(array, pltpu.HBM)
+            for array in (
+                queries[0], keys[0], values[0], out_proj.T, depth_proj.T, code_table,
+                code_ids[0].T, depth_cotangent[0],
+            )
+        )
     )
+    gq, gk, gv, gop = write_out(gq, gk, gv, gop)
     return gq[None], gk[None], gv[None], gop.T
 
 

time: 119 us -> 108 us (0.908)
  local copies, waits for them, and re-layouts: 10.1 us -> 0 us
    unnamed x20 -> x0, local copies, waits for them, and re-layouts: 10.1 us -> none
    pallas_call x1, Pallas kernels: 108 us -> 106 us  [on_device(): pl.pallas_call(functools.partial(kernel, scale), out_shape=(jax.ShapeDtyp...]
    pallas_call x0 -> x1, Pallas kernels: none -> 1.21 us  [write_out(): pl.pallas_call(out_kernel, out_shape=tuple((jax.ShapeDtypeStruct(a.shape,...]
where the time goes in v3:
time: 108 us
  Pallas kernels  107 us (99%)
    pallas_call x1, Pallas kernels, on_device(): pl.pallas_call(functools.partial(kernel, scale), out_shape=(jax.ShapeDtyp...  106 us

profile of v3, /device:TPU:1, one launch (start us, length us, event | category | flops | bytes accessed | tf_op | source)
XLA Modules:
  0.0 107.6 jit_solution(5685069071509777727)
XLA Ops:
  0.6 105.7 %fused_step.1 = (bf16[512,512]{1,0:T(8,128)(2,1)S(1)}, bf16[512,512]{1,0:T(8,128)(2,1)S(1)}, bf16[512,512]{1,0:T(8,128)(2,1)S(1)}, f32[64,512]{1,0:T(8,128)S(1)}) custom-call(bf16[512,512]{1,0:T(8,128)(2,1)} %bitcast.13, bf16[512,512]{1,0:T(8,128)(2,1)} %bitcast.14, bf16[512,512]{1,0:T(8,128)(2,1)} %bitcast.15, bf16[64,512]{1,0:T(8,128)(2,1)} %bitcast.17, ...), custom_call_target="tpu_custom_call" | custom-call | tf_op jit(solution)/shard_map/fused_step/pallas_call | solution.py:663
  106.3 1.2 %write_out.1 = (bf16[512,512]{1,0:T(8,128)(2,1)}, bf16[512,512]{1,0:T(8,128)(2,1)}, bf16[512,512]{1,0:T(8,128)(2,1)}, f32[64,512]{1,0:T(8,128)}) custom-call(bf16[512,512]{1,0:T(8,128)(2,1)S(1)} %get-tuple-element.12.refs_0_, bf16[512,512]{1,0:T(8,128)(2,1)S(1)} %get-tuple-element.13.refs_1_, bf16[512,512]{1,0:T(8,128)(2,1)S(1)} %get-tuple-element.14.refs_2_, ...), custom_call_target="tpu_custom_call" | custom-call | tf_op jit(solution)/shard_map/write_out/pallas_call | solution.py:646

commit v4 on v3

--- a/solution.py
+++ b/solution.py
@@ -62,7 +62,7 @@
     mix, ra1, rb1, ra2, rb2, ray, rar, raf, rbr, rbf, yb, sb1, sb2,
     mixed, emb, gpre,
     gb, gra, grb,
-    ga, wg, wgr, zsend, zrecv, y_own, y_recv, o_own, o_recv,
+    ga, wg, wgr, zsend, zrecv, y_own, y_recv,
     send_sems, recv_sems,
 ):
     seq, head, z = lax.axis_index("seq"), lax.axis_index("head"), lax.axis_index("dp")
@@ -92,11 +92,12 @@
     zp2, zm2 = dev(z_=at_z(2)), dev(z_=at_z(-2))
     mate = dev(c_=1 - c)
     pair = dev(y_=2 * yh + 1 - yl)
+    cross = dev(y_=2 * yh + 1 - yl, c_=1 - c)
     cf, ylf = c.astype(F32), yl.astype(F32)
     go = Copies(send_sems, recv_sems)
 
     barrier = pltpu.get_barrier_semaphore()
-    for other in (xp, xm, yp, ym, zp, zm, zp2, zm2, mate):
+    for other in (xp, xm, yp, ym, zp, zm, zp2, zm2, mate, cross):
         pl.semaphore_signal(barrier, inc=1, device_id=other, device_id_type=pl.DeviceIdType.MESH)
 
     def hs(i):
@@ -125,7 +126,7 @@
         s_own[i] = dot_tn(k_ref[:, hs(i)], v_ref[:, hs(i)]).astype(BF16)
     for load in loads[4:]:
         load.wait()
-    pl.semaphore_wait(barrier, 9)
+    pl.semaphore_wait(barrier, 10)
 
     state_copy = go.send(s_own, s_recv, mate)
     own_p = op_ref.at[pl.ds(pl.multiple_of(mine, 32), 32), :]
@@ -382,32 +383,32 @@
     near = Plane(0)
     relay_p(2)
     finish_attended()
+    relay_w(3)
     near.second()
     for rel in (-1, -2, 1, 2, -3, 3, 4):
         to_mate[rel].wait_recv()
     mnear = Reduce(0)
-    relay_w(3)
+    relay_p(3)
     near.third()
-    relay_p(3)
     mnear.second()
     for rel in (-7, -8, 7):
         w_came[rel].wait_recv()
     far = Plane(1)
-    mnear.third()
     for rel in (-7, -8, 7):
         p_came[rel].wait_recv()
         p_mate(rel)
+    near.fourth()
     for rel in (-4, -5, -6, 5, 6, -7, -8, 7):
         to_mate[rel].wait_recv()
     mfar = Reduce(1)
+    mnear.third()
     far.second()
-    mnear.fourth()
-    near.fourth()
     mfar.second()
     far.third()
+    mnear.fourth()
+    near.fifth()
+    mfar.third()
     mnear.fifth()
-    mfar.third()
-    near.fifth()
     mfar.fourth()
     far.fourth()
     mfar.fifth()
@@ -554,18 +555,19 @@
             came[n] = go.send(zsend.at[n, m], zrecv.at[n, m], device)
 
     spread_far = Spread(1)
+    spread_far.second()
     spread_near = Spread(0)
-    spread_far.second()
+    spread_far.third()
     spread_near.second()
-    spread_far.third()
+    spread_far.fourth()
     spread_near.third()
-    spread_far.fourth()
     spread_far.fifth()
     wg_far = halves(1)
     spread_near.fourth()
     wg_far.wait_recv()
     chain_step(0)
     spread_near.fifth()
+    chain_step(1)
     wg_near = halves(0)
 
     for j in range(2):
@@ -602,17 +604,16 @@
         ).astype(BF16)
         gv_ref[bot, hs(i)] = (scale * (dot_tn(sc[i, 2], a1_) + dot(k1_, b))).astype(BF16)
 
-    chain_step(1)
     back_copy.wait_recv()
     bt_own[...] = (b_own[...].astype(F32) + b_recv[...].astype(F32)).astype(BF16)
     back_pair = go.send(bt_own, bt_recv, pair)
     wg_near.wait_recv()
+    chain_step(2)
     back_pair.wait_recv()
     b_in[...] = (
         (1.0 - cf) * b_recv[...].astype(F32) + (1.0 - ylf) * bt_recv[...].astype(F32)
     ).astype(BF16)
     backward(0)
-    chain_step(2)
     backward(1)
     backward(2)
     chain_step(3)
@@ -622,13 +623,15 @@
         came[n].wait_recv()
         total = total + zrecv[n, length - 1].astype(F32)
     y_own[...] = total.astype(BF16)
-    y_copy = go.send(y_own, y_recv, pair)
-    y_copy.wait_recv()
-    o_own[...] = y_own[...].astype(F32) + y_recv[...].astype(F32)
-    o_copy = go.send(o_own, o_recv, mate)
-    go_ref[pl.ds(pl.multiple_of(mine, 32), 32), :] = o_own[...]
-    o_copy.wait_recv()
-    go_ref[pl.ds(pl.multiple_of(32 - mine, 32), 32), :] = o_recv[...]
+    last = [go.send(y_own, y_recv.at[n], device) for n, device in enumerate((pair, mate, cross))]
+    for copy in last:
+        copy.wait_recv()
+    go_ref[pl.ds(pl.multiple_of(mine, 32), 32), :] = (
+        y_own[...].astype(F32) + y_recv[0].astype(F32)
+    )
+    go_ref[pl.ds(pl.multiple_of(32 - mine, 32), 32), :] = (
+        y_recv[1].astype(F32) + y_recv[2].astype(F32)
+    )
     go.drain()
 
 
@@ -688,7 +691,7 @@
             vm((4, 2, 2, 32, 1024)), vm((2, 2, 4, 32, 256)), vm((2, 2, 32, 256)),
             vm((512, 512)), vm((16, 2, 32, 512)), vm((16, 32, 512)),
             vm((4, 4, 32, 512)), vm((4, 4, 32, 512)),
-            vm((32, 512)), vm((32, 512)), vm((32, 512), F32), vm((32, 512), F32),
+            vm((32, 512)), vm((3, 32, 512)),
             pltpu.SemaphoreType.DMA((N_COPIES,)),
             pltpu.SemaphoreType.DMA((N_COPIES,)),
         ],

time: 108 us -> 103 us (0.954)
  Pallas kernels: 107 us -> 103 us
    pallas_call x1, Pallas kernels: 106 us -> 101 us  [on_device(): pl.pallas_call(functools.partial(kernel, scale), out_shape=(jax.ShapeDtyp...]
where the time goes in v4:
time: 103 us
  Pallas kernels  103 us (100%)
    pallas_call x1, Pallas kernels, on_device(): pl.pallas_call(functools.partial(kernel, scale), out_shape=(jax.ShapeDtyp...  101 us

profile of v4, /device:TPU:1, one launch (start us, length us, event | category | flops | bytes accessed | tf_op | source)
XLA Modules:
  0.0 103.2 jit_solution(15367769385281742189)
XLA Ops:
  0.6 101.4 %fused_step.1 = (bf16[512,512]{1,0:T(8,128)(2,1)S(1)}, bf16[512,512]{1,0:T(8,128)(2,1)S(1)}, bf16[512,512]{1,0:T(8,128)(2,1)S(1)}, f32[64,512]{1,0:T(8,128)S(1)}) custom-call(bf16[512,512]{1,0:T(8,128)(2,1)} %bitcast.13, bf16[512,512]{1,0:T(8,128)(2,1)} %bitcast.14, bf16[512,512]{1,0:T(8,128)(2,1)} %bitcast.15, bf16[64,512]{1,0:T(8,128)(2,1)} %bitcast.17, ...), custom_call_target="tpu_custom_call" | custom-call | tf_op jit(solution)/shard_map/fused_step/pallas_call | solution.py:666
  102.0 1.2 %write_out.1 = (bf16[512,512]{1,0:T(8,128)(2,1)}, bf16[512,512]{1,0:T(8,128)(2,1)}, bf16[512,512]{1,0:T(8,128)(2,1)}, f32[64,512]{1,0:T(8,128)}) custom-call(bf16[512,512]{1,0:T(8,128)(2,1)S(1)} %get-tuple-element.12.refs_0_, bf16[512,512]{1,0:T(8,128)(2,1)S(1)} %get-tuple-element.13.refs_1_, bf16[512,512]{1,0:T(8,128)(2,1)S(1)} %get-tuple-element.14.refs_2_, ...), custom_call_target="tpu_custom_call" | custom-call | tf_op jit(solution)/shard_map/write_out/pallas_call | solution.py:649

commit v5 on v4

--- a/solution.py
+++ b/solution.py
@@ -106,8 +106,8 @@
     loads = [
         pltpu.make_async_copy(src, dst, load_sems.at[n])
         for n, (src, dst) in enumerate((
-            (dp_in, dp_ref), (tab_in, tab_ref), (k_in, k_ref), (v_in, v_ref),
-            (q_in, q_ref), (op_in, op_ref), (ids_in, ids_ref), (cot_in, cot_ref),
+            (dp_in, dp_ref), (tab_in, tab_ref), (op_in, op_ref), (k_in, k_ref),
+            (v_in, v_ref), (q_in, q_ref), (ids_in, ids_ref), (cot_in, cot_ref),
         ))
     ]
     for load in loads:
@@ -121,14 +121,8 @@
         rows8 = (dp_ref[:, qown] if a == 0 else tab_ref[a - 1, :, qown]).astype(F32)
         wz[3, a] = jnp.concatenate([rows8[:, :128], rows8[:, 128:]], axis=0).astype(BF16)
     loads[2].wait()
-    loads[3].wait()
-    for i in range(4):
-        s_own[i] = dot_tn(k_ref[:, hs(i)], v_ref[:, hs(i)]).astype(BF16)
-    for load in loads[4:]:
-        load.wait()
     pl.semaphore_wait(barrier, 10)
 
-    state_copy = go.send(s_own, s_recv, mate)
     own_p = op_ref.at[pl.ds(pl.multiple_of(mine, 32), 32), :]
 
     w_came, p_came, to_mate = {}, {}, {}
@@ -152,6 +146,11 @@
         send_wz(0, hop, device)
     for hop, device in around:
         send_p(0, hop, device)
+    for load in loads[3:]:
+        load.wait()
+    for i in range(4):
+        s_own[i] = dot_tn(k_ref[:, hs(i)], v_ref[:, hs(i)]).astype(BF16)
+    state_copy = go.send(s_own, s_recv, mate)
     proj[3] = op_ref[...].reshape(2, 32, 512)
 
     def relay_w(j):
@@ -277,100 +276,109 @@
             w_mate.append(same(self.bx(at_x(2), 32, 32), mate))
 
     class Reduce:
-        def __init__(self, group):
-            self.g, self.a0, self.b0 = group, 512 * group, 512 * group + 256
-            self.block(2 * group + 1)
-            b = pl.ds(self.b0, 256)
+        def __init__(self, g, a0, b0, w):
+            self.g, self.a0, self.b0, self.w = g, a0, b0, w
+            self.c = pl.ds(0, w)
+            self.block(b0)
+            b = pl.ds(b0, w)
             self.y1 = (
-                go.send(mix.at[:, 1 - yh, 0, :, b], rbr.at[group, 0], yp),
-                go.send(mix.at[:, 1 - yh, 1, :, b], rbr.at[group, 1], ym),
-            )
-            self.block(2 * group)
-            a = pl.ds(self.a0, 256)
+                go.send(mix.at[:, 1 - yh, 0, :, b], rbr.at[g, 0, :, :, self.c], yp),
+                go.send(mix.at[:, 1 - yh, 1, :, b], rbr.at[g, 1, :, :, self.c], ym),
+            )
+            self.block(a0)
+            a = pl.ds(a0, w)
             self.x1 = (
-                go.send(mix.at[at_x(2), 0, :, :, a], ra1.at[group], xp),
-                go.send(mix.at[at_x(2), 1, :, :, a], rb1.at[group], xm),
-            )
-
-        def block(self, j):
-            part = dot_nt(att[...], proj[4 * j:4 * j + 4].reshape(256, 512))
-            mix[:, :, :, :, 256 * j:256 * j + 256] = part.astype(BF16).reshape(4, 2, 2, 32, 256)
+                go.send(mix.at[at_x(2), 0, :, :, a], ra1.at[g, :, :, self.c], xp),
+                go.send(mix.at[at_x(2), 1, :, :, a], rb1.at[g, :, :, self.c], xm),
+            )
+
+        def block(self, col):
+            s0, n = col // 64, self.w // 64
+            part = dot_nt(att[...], proj[s0:s0 + n].reshape(self.w, 512))
+            mix[:, :, :, :, col:col + self.w] = part.astype(BF16).reshape(4, 2, 2, 32, self.w)
 
         def second(self):
-            g, al = self.g, slice(self.a0, self.a0 + 256)
+            g, w, al = self.g, self.w, slice(self.a0, self.a0 + self.w)
             for copy in self.y1:
                 copy.wait_recv()
-            self.y2 = (
-                go.send(rbr.at[g, 0], rbf.at[g, 0], yp), go.send(rbr.at[g, 1], rbf.at[g, 1], ym)
+            self.y2 = tuple(
+                go.send(rbr.at[g, n, :, :, self.c], rbf.at[g, n, :, :, self.c], device)
+                for n, device in ((0, yp), (1, ym))
             )
             for copy in self.x1:
                 copy.wait_recv()
             mix[at_x(1), 0, :, :, al] = (
-                mix[at_x(1), 0, :, :, al].astype(F32) + ra1[g].astype(F32)
+                mix[at_x(1), 0, :, :, al].astype(F32) + ra1[g, :, :, :w].astype(F32)
             ).astype(BF16)
             mix[at_x(-1), 1, :, :, al] = (
-                mix[at_x(-1), 1, :, :, al].astype(F32) + rb1[g].astype(F32)
+                mix[at_x(-1), 1, :, :, al].astype(F32) + rb1[g, :, :, :w].astype(F32)
             ).astype(BF16)
-            a = pl.ds(self.a0, 256)
+            a = pl.ds(self.a0, w)
             self.x2 = (
-                go.send(mix.at[at_x(1), :, :, :, a], ra2.at[g], xp),
-                go.send(mix.at[at_x(-1), :, :, :, a], rb2.at[g], xm),
+                go.send(mix.at[at_x(1), :, :, :, a], ra2.at[g, :, :, :, self.c], xp),
+                go.send(mix.at[at_x(-1), :, :, :, a], rb2.at[g, :, :, :, self.c], xm),
             )
 
         def third(self):
-            g, al, be = self.g, slice(self.a0, self.a0 + 256), slice(self.b0, self.b0 + 256)
+            g, w = self.g, self.w
+            al, be = slice(self.a0, self.a0 + w), slice(self.b0, self.b0 + w)
             for copy in self.y2:
                 copy.wait_recv()
             for hf in range(2):
-                yb[g, :, hf] = (
-                    mix[:, yh, hf, :, be].astype(F32) + rbf[g, hf].astype(F32)
+                yb[g, :, hf, :, :w] = (
+                    mix[:, yh, hf, :, be].astype(F32) + rbf[g, hf, :, :, :w].astype(F32)
                 ).astype(BF16)
-            self.bx1 = (
-                go.send(yb.at[g, at_x(2), 0], sb1.at[g, 0], xp),
-                go.send(yb.at[g, at_x(2), 1], sb1.at[g, 1], xm),
+            self.bx1 = tuple(
+                go.send(yb.at[g, at_x(2), n, :, self.c], sb1.at[g, n, :, self.c], device)
+                for n, device in ((0, xp), (1, xm))
             )
             for copy in self.x2:
                 copy.wait_recv()
-            ray[g] = (
+            ray[g, :, :, :w] = (
                 mix[x, 1 - yh, :, :, al].astype(F32)
-                + ra2[g, 1 - yh].astype(F32)
-                + rb2[g, 1 - yh].astype(F32)
+                + ra2[g, 1 - yh, :, :, :w].astype(F32)
+                + rb2[g, 1 - yh, :, :, :w].astype(F32)
             ).astype(BF16)
-            self.ay1 = (
-                go.send(ray.at[g, 0], rar.at[g, 0], yp), go.send(ray.at[g, 1], rar.at[g, 1], ym)
+            self.ay1 = tuple(
+                go.send(ray.at[g, n, :, self.c], rar.at[g, n, :, self.c], device)
+                for n, device in ((0, yp), (1, ym))
             )
             mixed[:, al] = (
                 mix[x, yh, :, :, al].astype(F32)
-                + ra2[g, yh].astype(F32)
-                + rb2[g, yh].astype(F32)
-            ).reshape(64, 256)
+                + ra2[g, yh, :, :, :w].astype(F32)
+                + rb2[g, yh, :, :, :w].astype(F32)
+            ).reshape(64, w)
 
         def fourth(self):
-            g = self.g
+            g, w = self.g, self.w
             for copy in self.bx1:
                 copy.wait_recv()
             for step, hf in ((1, 0), (-1, 1)):
-                yb[g, at_x(step), hf] = (
-                    yb[g, at_x(step), hf].astype(F32) + sb1[g, hf].astype(F32)
+                yb[g, at_x(step), hf, :, :w] = (
+                    yb[g, at_x(step), hf, :, :w].astype(F32) + sb1[g, hf, :, :w].astype(F32)
                 ).astype(BF16)
-            self.bx2 = (
-                go.send(yb.at[g, at_x(1)], sb2.at[g, 0], xp),
-                go.send(yb.at[g, at_x(-1)], sb2.at[g, 1], xm),
+            self.bx2 = tuple(
+                go.send(yb.at[g, at_x(step), :, :, self.c], sb2.at[g, n, :, :, self.c], device)
+                for n, step, device in ((0, 1, xp), (1, -1, xm))
             )
             for copy in self.ay1:
                 copy.wait_recv()
-            self.ay2 = (
-                go.send(rar.at[g, 0], raf.at[g, 0], yp), go.send(rar.at[g, 1], raf.at[g, 1], ym)
+            self.ay2 = tuple(
+                go.send(rar.at[g, n, :, self.c], raf.at[g, n, :, self.c], device)
+                for n, device in ((0, yp), (1, ym))
             )
 
         def fifth(self):
-            g, al, be = self.g, slice(self.a0, self.a0 + 256), slice(self.b0, self.b0 + 256)
+            g, w = self.g, self.w
+            al, be = slice(self.a0, self.a0 + w), slice(self.b0, self.b0 + w)
             for copy in self.ay2 + self.bx2:
                 copy.wait_recv()
-            mixed[:, al] = mixed[:, al] + raf[g].astype(F32).reshape(64, 256)
+            mixed[:, al] = mixed[:, al] + raf[g, :, :, :w].astype(F32).reshape(64, w)
             mixed[:, be] = (
-                yb[g, x].astype(F32) + sb2[g, 0].astype(F32) + sb2[g, 1].astype(F32)
-            ).reshape(64, 256)
+                yb[g, x, :, :, :w].astype(F32)
+                + sb2[g, 0, :, :, :w].astype(F32)
+                + sb2[g, 1, :, :, :w].astype(F32)
+            ).reshape(64, w)
 
     forward(0)
     pair_copy = pass_state()
@@ -387,7 +395,7 @@
     near.second()
     for rel in (-1, -2, 1, 2, -3, 3, 4):
         to_mate[rel].wait_recv()
-    mnear = Reduce(0)
+    mnear = Reduce(0, 0, 256, 256)
     relay_p(3)
     near.third()
     mnear.second()
@@ -400,7 +408,7 @@
     near.fourth()
     for rel in (-4, -5, -6, 5, 6, -7, -8, 7):
         to_mate[rel].wait_recv()
-    mfar = Reduce(1)
+    mfar = Reduce(1, 512, 768, 256)
     mnear.third()
     far.second()
     mfar.second()
@@ -471,11 +479,12 @@
     gb[x, yh] = grad.astype(BF16).reshape(2, 32, 1024)
 
     class Spread:
-        def __init__(self, group):
-            self.g, self.a, self.b = group, pl.ds(512 * group, 256), pl.ds(512 * group + 256, 256)
+        def __init__(self, group, a0, b0, w):
+            self.a, self.b = pl.ds(a0, w), pl.ds(b0, w)
+            self.ra, self.rb = gra.at[group, :, :, :, pl.ds(0, w)], grb.at[group, :, :, pl.ds(0, w)]
             self.y1 = (
-                go.send(gb.at[x, yh, 0, :, self.b], grb.at[group, 0], yp),
-                go.send(gb.at[x, yh, 1, :, self.b], grb.at[group, 1], ym),
+                go.send(gb.at[x, yh, 0, :, self.b], self.rb.at[0], yp),
+                go.send(gb.at[x, yh, 1, :, self.b], self.rb.at[1], ym),
             )
             own = gb.at[x, yh, :, :, self.a]
             self.x1 = (same(own, xp), same(own, xm))
@@ -484,8 +493,8 @@
             for copy in self.y1:
                 copy.wait_recv()
             self.y2 = (
-                go.send(grb.at[self.g, 0], gb.at[x, at_y(-1) // 2, 0, :, self.b], yp),
-                go.send(grb.at[self.g, 1], gb.at[x, at_y(1) // 2, 1, :, self.b], ym),
+                go.send(self.rb.at[0], gb.at[x, at_y(-1) // 2, 0, :, self.b], yp),
+                go.send(self.rb.at[1], gb.at[x, at_y(1) // 2, 1, :, self.b], ym),
             )
             for copy in self.x1:
                 copy.wait_recv()
@@ -502,8 +511,8 @@
             for copy in self.x2:
                 copy.wait_recv()
             self.ay1 = (
-                go.send(gb.at[:, yh, 0, :, self.a], gra.at[self.g, 0], yp),
-                go.send(gb.at[:, yh, 1, :, self.a], gra.at[self.g, 1], ym),
+                go.send(gb.at[:, yh, 0, :, self.a], self.ra.at[0], yp),
+                go.send(gb.at[:, yh, 1, :, self.a], self.ra.at[1], ym),
             )
 
         def fourth(self):
@@ -516,23 +525,19 @@
             for copy in self.ay1:
                 copy.wait_recv()
             self.ay2 = (
-                go.send(gra.at[self.g, 0], gb.at[:, at_y(-1) // 2, 0, :, self.a], yp),
-                go.send(gra.at[self.g, 1], gb.at[:, at_y(1) // 2, 1, :, self.a], ym),
+                go.send(self.ra.at[0], gb.at[:, at_y(-1) // 2, 0, :, self.a], yp),
+                go.send(self.ra.at[1], gb.at[:, at_y(1) // 2, 1, :, self.a], ym),
             )
 
         def fifth(self):
             for copy in self.bx2 + self.ay2:
                 copy.wait_recv()
 
-    def weight_grad(j):
-        block = gb[:, :, :, :, 256 * j:256 * j + 256].reshape(512, 256)
-        wg[4 * j:4 * j + 4] = dot_tn(block, att[...]).astype(BF16).reshape(4, 2, 32, 512)
-
-    def halves(group):
-        weight_grad(2 * group)
-        weight_grad(2 * group + 1)
-        rows8 = pl.ds(8 * group, 8)
-        return go.send(wg.at[rows8, 1 - c], wgr.at[rows8], mate)
+    def weight_grad(s0, n):
+        block = gb[:, :, :, :, 64 * s0:64 * (s0 + n)].reshape(512, 64 * n)
+        wg[s0:s0 + n] = dot_tn(block, att[...]).astype(BF16).reshape(n, 2, 32, 512)
+        rows_n = pl.ds(s0, n)
+        return go.send(wg.at[rows_n, 1 - c], wgr.at[rows_n], mate)
 
     def own_chunk(rel):
         return wg[slot(rel), c].astype(F32) + wgr[slot(rel)].astype(F32)
@@ -554,21 +559,29 @@
             device = {2: zp2, 1: zp, -1: zm, -2: zm2}[max(-2, min(2, dist))]
             came[n] = go.send(zsend.at[n, m], zrecv.at[n, m], device)
 
-    spread_far = Spread(1)
+    spread_far = Spread(2, 640, 768, 128)
+    spread_mid = Spread(1, 512, 896, 128)
     spread_far.second()
-    spread_near = Spread(0)
+    spread_mid.second()
     spread_far.third()
+    spread_mid.third()
+    spread_near = Spread(0, 0, 256, 256)
+    spread_far.fourth()
+    spread_mid.fourth()
     spread_near.second()
-    spread_far.fourth()
+    spread_far.fifth()
+    wg_far = weight_grad(10, 4)
+    spread_mid.fifth()
+    wg_mid = (weight_grad(8, 2), weight_grad(14, 2))
     spread_near.third()
-    spread_far.fifth()
-    wg_far = halves(1)
-    spread_near.fourth()
     wg_far.wait_recv()
     chain_step(0)
+    spread_near.fourth()
+    for copy in wg_mid:
+        copy.wait_recv()
+    chain_step(1)
     spread_near.fifth()
-    chain_step(1)
-    wg_near = halves(0)
+    wg_near = (weight_grad(0, 4), weight_grad(4, 4))
 
     for j in range(2):
         total = None
@@ -607,23 +620,24 @@
     back_copy.wait_recv()
     bt_own[...] = (b_own[...].astype(F32) + b_recv[...].astype(F32)).astype(BF16)
     back_pair = go.send(bt_own, bt_recv, pair)
-    wg_near.wait_recv()
+    for copy in wg_near:
+        copy.wait_recv()
     chain_step(2)
+    chain_step(3)
     back_pair.wait_recv()
     b_in[...] = (
         (1.0 - cf) * b_recv[...].astype(F32) + (1.0 - ylf) * bt_recv[...].astype(F32)
     ).astype(BF16)
     backward(0)
     backward(1)
-    backward(2)
-    chain_step(3)
-    backward(3)
     total = own_chunk(0)
     for n, (first, length) in enumerate(chains):
         came[n].wait_recv()
         total = total + zrecv[n, length - 1].astype(F32)
     y_own[...] = total.astype(BF16)
     last = [go.send(y_own, y_recv.at[n], device) for n, device in enumerate((pair, mate, cross))]
+    backward(2)
+    backward(3)
     for copy in last:
         copy.wait_recv()
     go_ref[pl.ds(pl.multiple_of(mine, 32), 32), :] = (
@@ -682,13 +696,13 @@
             state, state, state, state, state,
             vm((4, 3, 256, 256)), vm((512, 512), F32), vm((512, 512)),
             vm((4, 2, 2, 32, 1024)),
-            vm((2, 2, 32, 256)), vm((2, 2, 32, 256)),
-            vm((2, 2, 2, 32, 256)), vm((2, 2, 2, 32, 256)),
-            vm((2, 2, 32, 256)), vm((2, 2, 32, 256)), vm((2, 2, 32, 256)),
-            vm((2, 2, 4, 32, 256)), vm((2, 2, 4, 32, 256)),
-            vm((2, 4, 2, 32, 256)), vm((2, 2, 32, 256)), vm((2, 2, 2, 32, 256)),
+            vm((3, 2, 32, 256)), vm((3, 2, 32, 256)),
+            vm((3, 2, 2, 32, 256)), vm((3, 2, 2, 32, 256)),
+            vm((3, 2, 32, 256)), vm((3, 2, 32, 256)), vm((3, 2, 32, 256)),
+            vm((3, 2, 4, 32, 256)), vm((3, 2, 4, 32, 256)),
+            vm((3, 4, 2, 32, 256)), vm((3, 2, 32, 256)), vm((3, 2, 2, 32, 256)),
             vm((64, 1024), F32), vm((2, 64, 1024), F32), vm((64, 1024), F32),
-            vm((4, 2, 2, 32, 1024)), vm((2, 2, 4, 32, 256)), vm((2, 2, 32, 256)),
+            vm((4, 2, 2, 32, 1024)), vm((3, 2, 4, 32, 256)), vm((3, 2, 32, 256)),
             vm((512, 512)), vm((16, 2, 32, 512)), vm((16, 32, 512)),
             vm((4, 4, 32, 512)), vm((4, 4, 32, 512)),
             vm((32, 512)), vm((3, 32, 512)),

time: 103 us -> 102 us (level)
  Pallas kernels: 103 us -> 101 us
    pallas_call x1, Pallas kernels: 101 us -> 99.7 us  [on_device(): pl.pallas_call(functools.partial(kernel, scale), out_shape=(jax.ShapeDtyp...]
where the time goes in v5:
time: 102 us
  Pallas kernels  101 us (99%)
    pallas_call x1, Pallas kernels, on_device(): pl.pallas_call(functools.partial(kernel, scale), out_shape=(jax.ShapeDtyp...  99.7 us

profile of v5, /device:TPU:1, one launch (start us, length us, event | category | flops | bytes accessed | tf_op | source)
XLA Modules:
  0.0 101.5 jit_solution(11807642472676815371)
XLA Ops:
  0.6 99.7 %fused_step.1 = (bf16[512,512]{1,0:T(8,128)(2,1)S(1)}, bf16[512,512]{1,0:T(8,128)(2,1)S(1)}, bf16[512,512]{1,0:T(8,128)(2,1)S(1)}, f32[64,512]{1,0:T(8,128)S(1)}) custom-call(bf16[512,512]{1,0:T(8,128)(2,1)} %bitcast.13, bf16[512,512]{1,0:T(8,128)(2,1)} %bitcast.14, bf16[512,512]{1,0:T(8,128)(2,1)} %bitcast.15, bf16[64,512]{1,0:T(8,128)(2,1)} %bitcast.17, ...), custom_call_target="tpu_custom_call" | custom-call | tf_op jit(solution)/shard_map/fused_step/pallas_call | solution.py:680
  100.3 1.2 %write_out.1 = (bf16[512,512]{1,0:T(8,128)(2,1)}, bf16[512,512]{1,0:T(8,128)(2,1)}, bf16[512,512]{1,0:T(8,128)(2,1)}, f32[64,512]{1,0:T(8,128)}) custom-call(bf16[512,512]{1,0:T(8,128)(2,1)S(1)} %get-tuple-element.12.refs_0_, bf16[512,512]{1,0:T(8,128)(2,1)S(1)} %get-tuple-element.13.refs_1_, bf16[512,512]{1,0:T(8,128)(2,1)S(1)} %get-tuple-element.14.refs_2_, ...), custom_call_target="tpu_custom_call" | custom-call | tf_op jit(solution)/shard_map/write_out/pallas_call | solution.py:663

commit v6 on v5

--- a/solution.py
+++ b/solution.py
@@ -397,28 +397,28 @@
         to_mate[rel].wait_recv()
     mnear = Reduce(0, 0, 256, 256)
     relay_p(3)
+    for rel in (-7, -8, 7):
+        w_came[rel].wait_recv()
+    far = Plane(1)
     near.third()
     mnear.second()
     for rel in (-7, -8, 7):
-        w_came[rel].wait_recv()
-    far = Plane(1)
-    for rel in (-7, -8, 7):
         p_came[rel].wait_recv()
         p_mate(rel)
+    far.second()
     near.fourth()
     for rel in (-4, -5, -6, 5, 6, -7, -8, 7):
         to_mate[rel].wait_recv()
     mfar = Reduce(1, 512, 768, 256)
+    far.third()
     mnear.third()
-    far.second()
     mfar.second()
-    far.third()
     mnear.fourth()
     near.fifth()
     mfar.third()
+    far.fourth()
     mnear.fifth()
     mfar.fourth()
-    far.fourth()
     mfar.fifth()
     far.fifth()
     for copy in w_mate:

time: 102 us -> 103 us (level)
  no operation moved by 1% of the time
where the time goes in v6:
time: 103 us
  Pallas kernels  102 us (99%)
    pallas_call x1, Pallas kernels, on_device(): pl.pallas_call(functools.partial(kernel, scale), out_shape=(jax.ShapeDtyp...  101 us

profile of v6, /device:TPU:1, one launch (start us, length us, event | category | flops | bytes accessed | tf_op | source)
XLA Modules:
  0.0 102.5 jit_solution(10908197657920676888)
XLA Ops:
  0.6 100.7 %fused_step.1 = (bf16[512,512]{1,0:T(8,128)(2,1)S(1)}, bf16[512,512]{1,0:T(8,128)(2,1)S(1)}, bf16[512,512]{1,0:T(8,128)(2,1)S(1)}, f32[64,512]{1,0:T(8,128)S(1)}) custom-call(bf16[512,512]{1,0:T(8,128)(2,1)} %bitcast.13, bf16[512,512]{1,0:T(8,128)(2,1)} %bitcast.14, bf16[512,512]{1,0:T(8,128)(2,1)} %bitcast.15, bf16[64,512]{1,0:T(8,128)(2,1)} %bitcast.17, ...), custom_call_target="tpu_custom_call" | custom-call | tf_op jit(solution)/shard_map/fused_step/pallas_call | solution.py:680
  101.3 1.2 %write_out.1 = (bf16[512,512]{1,0:T(8,128)(2,1)}, bf16[512,512]{1,0:T(8,128)(2,1)}, bf16[512,512]{1,0:T(8,128)(2,1)}, f32[64,512]{1,0:T(8,128)}) custom-call(bf16[512,512]{1,0:T(8,128)(2,1)S(1)} %get-tuple-element.12.refs_0_, bf16[512,512]{1,0:T(8,128)(2,1)S(1)} %get-tuple-element.13.refs_1_, bf16[512,512]{1,0:T(8,128)(2,1)S(1)} %get-tuple-element.14.refs_2_, ...), custom_call_target="tpu_custom_call" | custom-call | tf_op jit(solution)/shard_map/write_out/pallas_call | solution.py:663
